TPU v7x, 256 devices: a whole 4x4x8 slice. The times are simulated.
256 devices in a mesh: space: 32 (over y, x, z_hi), band: 8 (over z_lo, core).
Axes of the slice: x: 4, y: 4, z: 8 (z_hi: 2, z_lo: 4; z = z_hi * 4 + z_lo), core: 2. Of those that a mesh axis runs over, the one named last changes fastest.
Arguments:
- orbitals: float32 [64, 192, 32, 128], P('band', 'space'), may hold values from -18 to 18
- previous: float32 [64, 192, 32, 128], P('band', 'space'), may hold values from -18 to 18
- potential: float32 [192, 32, 128], P('space'), may hold values from -4 to 4
- projectors: bfloat16 [128, 9, 6, 32, 128], P('space'), may hold values from -0.1875 to 0.1875
- strengths: float32 [128, 9], replicated, may hold values from -3 to 3
- atom_planes: int32 [128], replicated, may hold values from 0 to 191, as said below
Outputs:
- filtered: bfloat16 [64, 192, 32, 128], P('band', 'space')
- margin: float32 [64, 64], P('space', 'band')
- projection: float32 [64, 64], P('space', 'band')
Inputs may be any that keep to these rules, and one draw needn't show every extreme that they name: `atom_planes`: entry a is the first plane of atom a's box of 6 planes. In each aligned block of 4 entries (block s) every box starts at one of the planes s * 6 to s * 6 + 5, and in every block one atom starts at the first of these planes and another at the last.
All inputs are finite; a program needn't handle non-finite values.
Results may differ from a plain program's by a relative error of at most 0.0065.
Values may be sent and summed in bfloat16 or wider, within the bound.
A program may use at most 192 MiB of HBM per device.

v0:
```python
import jax
import jax.numpy as jnp
from jax import lax
from jax.sharding import PartitionSpec as P

HALO = 6
BOX = 6
NPJ = 9


stencil_weights = (
    -5369.0 / 1800.0,
    12.0 / 7.0,
    -15.0 / 56.0,
    10.0 / 189.0,
    -1.0 / 112.0,
    2.0 / 1925.0,
    -1.0 / 16632.0,
)
center = 5.5
halfwidth = 5.5


def with_halo(block, sides, width):
    for axis, dim in sides:
        count = lax.axis_size(axis)
        forward = [(i, i + 1) for i in range(count - 1)]
        forward.append((count - 1, 0))
        backward = [(target, source) for source, target in forward]
        low = lax.ppermute(
            lax.slice_in_dim(block, block.shape[dim] - width, None, axis=dim), axis, forward
        )
        high = lax.ppermute(lax.slice_in_dim(block, 0, width, axis=dim), axis, backward)
        block = jnp.concatenate([low, block, high], axis=dim)
    return block


def shifted(value, axis, steps):
    count = lax.axis_size(axis)
    pairs = [(source, (source + steps) % count) for source in range(count)]
    return lax.ppermute(value, axis, pairs)


def laplace_axis(field, axis):
    total = stencil_weights[0] * field
    for offset in range(1, HALO + 1):
        total = total + stencil_weights[offset] * (
            jnp.roll(field, offset, axis) + jnp.roll(field, -offset, axis)
        )
    return total


def place_table(first_planes, projector_block, base, window, total_planes):
    box_rows = jnp.arange(BOX, dtype=jnp.int32)
    planes_out = jnp.arange(window, dtype=jnp.int32)
    relative = (first_planes[:, None] + box_rows[None, :] - base) % total_planes
    placer = (planes_out[None, None, :] == relative[:, :, None]).astype(jnp.float32)
    return jnp.einsum(
        "apq,ajpyz->ajqyz",
        placer,
        projector_block.astype(jnp.float32),
        precision=lax.Precision.HIGHEST,
    )


def shards(orbitals, previous, potential, projectors, strengths, atom_planes):
    band_dev, slab_planes, cells_y, cells_z = orbitals.shape
    space_count = lax.axis_size("space")
    total_planes = slab_planes * space_count
    extended = with_halo(orbitals, (("space", 1),), HALO)
    along_x = stencil_weights[0] * orbitals
    for offset in range(1, HALO + 1):
        ahead = extended[:, HALO + offset : HALO + offset + slab_planes]
        behind = extended[:, HALO - offset : HALO - offset + slab_planes]
        along_x = along_x + stencil_weights[offset] * (ahead + behind)
    kinetic = -0.5 * (along_x + laplace_axis(orbitals, 2) + laplace_axis(orbitals, 3))
    device_index = lax.axis_index("space")
    atom_count = projectors.shape[0]
    own_start = device_index * atom_count
    own_planes = lax.dynamic_slice_in_dim(atom_planes, own_start, atom_count, 0)
    own_strengths = lax.dynamic_slice_in_dim(strengths, own_start, atom_count, 0)
    table = place_table(
        own_planes, projectors, device_index * slab_planes, slab_planes + HALO, total_planes
    )
    table_flat = table.reshape(atom_count * NPJ, -1)
    upper = extended[:, HALO:].reshape(band_dev, -1)
    coefficients = lax.dot_general(
        table_flat,
        upper,
        (((1,), (1,)), ((), ())),
        precision=lax.Precision.HIGHEST,
        preferred_element_type=jnp.float32,
    )
    weighted = coefficients * own_strengths.reshape(-1)[:, None]
    added = lax.dot_general(
        weighted,
        table_flat,
        (((0,), (0,)), ((), ())),
        precision=lax.Precision.HIGHEST,
        preferred_element_type=jnp.float32,
    )
    added = added.reshape(band_dev, slab_planes + HALO, cells_y, cells_z)
    arrived = shifted(added[:, slab_planes:].astype(jnp.bfloat16), "space", 1).astype(jnp.float32)
    padding = jnp.zeros((band_dev, slab_planes - HALO, cells_y, cells_z), jnp.float32)
    projected_term = added[:, :slab_planes] + jnp.concatenate([arrived, padding], 1)
    hamil = kinetic + potential[None] * orbitals + projected_term
    filtered = (2.0 / halfwidth * (hamil - center * orbitals) - previous).astype(jnp.bfloat16)
    scale = 1.0 / (slab_planes * space_count * cells_y * cells_z)
    filtered_flat = filtered.reshape(band_dev, -1)
    panel_flat = orbitals.astype(jnp.bfloat16).reshape(band_dev, -1)
    columns_right = jnp.concatenate([filtered_flat, panel_flat], 0)
    piece = lax.all_gather(filtered, "band", axis=0, tiled=True)
    rows = piece.reshape(piece.shape[0], -1)
    products = lax.dot_general(
        rows, columns_right, (((1,), (1,)), ((), ())), preferred_element_type=jnp.float32
    )
    partial_sums = products * scale
    shares = lax.psum_scatter(partial_sums, "space", scatter_dimension=0, tiled=True)
    margin = shares[:, :band_dev]
    projection = shares[:, band_dev:]
    return (filtered, margin, projection)


def solution(mesh):
    in_specs = (
        P("band", "space", None, None),
        P("band", "space", None, None),
        P("space", None, None),
        P("space", None, None, None, None),
        P(),
        P(),
    )
    out_specs = (P("band", "space", None, None), P("space", "band"), P("space", "band"))
    return jax.shard_map(shards, mesh=mesh, in_specs=in_specs, out_specs=out_specs, check_vma=False)
```

profile of v0, /device:TPU:32, one launch (start us, length us, event | category | flops | bytes accessed | tf_op | source)
XLA Modules:
  0.0 414.5 jit_solution(45234726132586732)
XLA Ops:
  7.2 1.7 copy.130
  8.9 6.4 %collective-permute-start.1 = (f32[8,6,32,128]{3,0,2,1:T(8,128)S(1)}, f32[8,6,32,128]{3,0,2,1:T(8,128)S(1)}, u32[]{:S(2)}, u32[]{:S(2)}) collective-permute-start(f32[8,6,32,128]{3,0,2,1:T(8,128)S(1)} %copy.130), channel_id=1, source_target_pairs={{0,8},{8,16},{16,24},{24,32},{32,40},{40,48},{48,56},{56,64},{64,7... | collective-permute-start | bytes 2359304 | tf_op jit(solution)/shard_map/ppermute | solution.py:30
  15.3 4.7 %collective-permute-start = (f32[8,6,32,128]{3,0,2,1:T(8,128)S(1)}, f32[8,6,32,128]{3,0,2,1:T(8,128)}, u32[]{:S(2)}, u32[]{:S(2)}) collective-permute-start(f32[8,6,32,128]{3,0,2,1:T(8,128)S(1)} %copy.130), channel_id=1, source_target_pairs={{8,0},{16,8},{24,16},{32,24},{40,32},{48,40},{56,48},{64,56},{72,6... | collective-permute-start | bytes 2359304 | tf_op jit(solution)/shard_map/ppermute | solution.py:33
  31.3 1.4 fusion.75
  32.8 1.5 fusion.72
  34.2 1.4 fusion.73
  41.3 1.5 fusion.66
  43.0 1.7 convolution_bitcast_fusion
  44.7 5.9 %copy.185 = f32[4,9,12,32,128]{4,3,2,1,0:T(8,128)} copy(f32[4,9,12,32,128]{4,2,3,1,0:T(8,128)S(1)} %convolution_bitcast_fusion) | data formatting | bytes 14155776 | tf_op jit(solution)/shard_map/apq,ajpyz->ajqyz/transpose | solution.py:58
  50.7 7.8 %reshape.53 = f32[36,49152]{1,0:T(8,128)} reshape(f32[4,9,12,32,128]{4,3,2,1,0:T(8,128)} %copy.185) | data formatting | bytes 14155776 | tf_op jit(solution)/shard_map/reshape | solution.py:85
  58.4 1.5 fusion.67
  60.2 4.7 %copy.194 = f32[5,8,384,128]{3,2,1,0:T(8,128)S(1)} copy(f32[5,8,384,128]{3,1,2,0:T(8,128)} %bitcast.38) | data formatting | bytes 15728640
  67.0 1.6 collective-permute-done.1
  69.1 3.2 collective-permute-done
  73.5 6.2 %fusion.9 = f32[36,8,1,1]{0,1,3,2:T(8,128)S(1)} fusion(f32[36,49152]{1,0:T(8,128)S(1)} %bitcast.40, f32[8,49152]{1,0:T(8,128)S(1)} %bitcast.43, f32[36]{0:T(128)S(1)} %mul.132), kind=kOutput, calls=%fused_computation.9 | convolution fusion | flops 169869600 | bytes 8652048 | tf_op jit(solution)/shard_map/dot_general | solution.py:87
  79.8 8.1 %fusion = f32[8,12,32,128]{3,0,2,1:T(8,128)S(1)} fusion(f32[36,8,1,1]{0,1,3,2:T(8,128)S(1)} %fusion.9, f32[12,32,128,36]{2,1,0,3:T(8,128)S(1)} %bitcast.41), kind=kOutput, calls=%fused_computation | convolution fusion | flops 169869312 | bytes 8651904 | tf_op jit(solution)/shard_map/dot_general | solution.py:95
  87.9 6.3 %collective-permute-start.2 = (bf16[8,6,32,128]{3,0,2,1:T(8,128)(2,1)S(1)}, bf16[8,6,32,128]{3,0,2,1:T(8,128)(2,1)}, u32[]{:S(2)}, u32[]{:S(2)}) collective-permute-start(bf16[8,6,32,128]{3,0,2,1:T(8,128)(2,1)S(1)} %slice.432), channel_id=1, source_target_pairs={{0,8},{8,16},{16,24},{24,32},{32,40},{40,48},{48,56},{56,64},{64,7... | collective-permute-start | bytes 1179656 | tf_op jit(solution)/shard_map/ppermute | solution.py:41
  94.2 1.5 fusion.65
  95.7 16.5 %collective-permute-done.2 = bf16[8,6,32,128]{3,0,2,1:T(8,128)(2,1)} collective-permute-done((bf16[8,6,32,128]{3,0,2,1:T(8,128)(2,1)S(1)}, bf16[8,6,32,128]{3,0,2,1:T(8,128)(2,1)}, u32[]{:S(2)}, u32[]{:S(2)}) %collective-permute-start.2) | collective-permute-done | bytes 393248 | tf_op jit(solution)/shard_map/ppermute | solution.py:41
  112.3 12.4 %fusion.14 = bf16[8,6,32,128]{3,0,2,1:T(8,128)(2,1)} fusion(f32[8,12,32,128]{3,0,2,1:T(8,128)S(1)} %fusion, f32[8,12,32,128]{3,0,2,1:T(8,128)S(1)} %get-tuple-element.60, f32[8,12,32,128]{3,0,2,1:T(8,128)S(1)} %constant_dynamic-update-slice_fusion, f32[8,6,31,128]{3,0,2,1:T(8,128)} %get-tuple-element.57, f32[8,6,1,128]{3,0,2,1:T(8,128)S(1)} %get-tuple-element.59, ...), kind=kLoop, calls=%fused_computation.16 | loop fusion | flops 18087936 | bytes 31555584 | tf_op jit(solution)/shard_map/convert_element_type | solution.py:107
  127.4 50.6 %all-gather.2.cloned.1.call-done = bf16[64,6,32,128]{3,0,2,1:T(8,128)(2,1)} async-done(((bf16[8,6,32,128]{3,0,2,1:T(8,128)(2,1)}), bf16[64,6,32,128]{3,0,2,1:T(8,128)(2,1)}) %all-gather.2.cloned.1.call-update) | async-done | bytes 3145744 | tf_op jit(solution)/shard_map/all_gather | solution.py:112
  178.0 3.9 copy.190
  181.9 1.8 fusion.6
  183.8 223.2 %all-reduce = f32[64,16]{1,0:T(8,128)S(1)} all-reduce(f32[64,16]{1,0:T(8,128)S(1)} %fusion.6), channel_id=2, replica_groups=mesh['space'=32,'band'=8] {'space'}, use_global_device_ids=true, to_apply=%region_0.1.clone | all-reduce | flops 1024 | bytes 8192
  (67 shorter events, 24.0 us)
Async XLA Ops:
  7.2 35.8 %copy-start = (bf16[4,9,6,32,128]{4,3,2,1,0:T(8,128)(2,1)S(1)}, bf16[4,9,6,32,128]{4,3,2,1,0:T(8,128)(2,1)}, u32[]{:S(2)}) copy-start(bf16[4,9,6,32,128]{4,3,2,1,0:T(8,128)(2,1)} %param.9) | copy-start | bytes 5308420
  7.2 170.8 %all-gather.2.cloned.1.call-start = ((), (), s32[]{:S(2)}) async-start(), calls=%async_computation | async-start | bytes 3538944 | tf_op jit(solution)/shard_map/all_gather | solution.py:112
  8.9 59.7 %collective-permute-start.1 = (f32[8,6,32,128]{3,0,2,1:T(8,128)S(1)}, f32[8,6,32,128]{3,0,2,1:T(8,128)S(1)}, u32[]{:S(2)}, u32[]{:S(2)}) collective-permute-start(f32[8,6,32,128]{3,0,2,1:T(8,128)S(1)} %copy.130), channel_id=1, source_target_pairs={{0,8},{8,16},{16,24},{24,32},{32,40},{40,48},{48,56},{56,64},{64,7... | collective-permute-start | bytes 2359304 | tf_op jit(solution)/shard_map/ppermute | solution.py:30
  15.3 57.0 %collective-permute-start = (f32[8,6,32,128]{3,0,2,1:T(8,128)S(1)}, f32[8,6,32,128]{3,0,2,1:T(8,128)}, u32[]{:S(2)}, u32[]{:S(2)}) collective-permute-start(f32[8,6,32,128]{3,0,2,1:T(8,128)S(1)} %copy.130), channel_id=1, source_target_pairs={{8,0},{16,8},{24,16},{32,24},{40,32},{48,40},{56,48},{64,56},{72,6... | collective-permute-start | bytes 2359304 | tf_op jit(solution)/shard_map/ppermute | solution.py:33
  41.3 1.5 copy-start.11
  58.4 1.5 copy-start.10
  64.8 8.7 %slice-start = ((s8[7864320]{0:T(1024)(128)(4,1)}), s8[4194304]{0:T(1024)(128)(4,1)S(1)}, s32[]{:S(2)}) async-start(s8[7864320]{0:T(1024)(128)(4,1)} %bitcast.39), calls=%async_computation.1 | async-start | bytes 8388608
  64.8 8.7 %slice-start.1 = ((s8[7864320]{0:T(1024)(128)(4,1)}), s8[3670016]{0:T(1024)(128)(4,1)S(1)}, s32[]{:S(2)}) async-start(s8[7864320]{0:T(1024)(128)(4,1)} %bitcast.39), calls=%async_computation.2 | async-start | bytes 7340032
  65.6 3.1 copy-start.2
  87.8 24.4 %copy-start.8 = (f32[8,6,32,126]{3,0,2,1:T(8,128)S(1)}, f32[8,6,32,126]{3,0,2,1:T(8,128)}, u32[]{:S(2)}) copy-start(f32[8,6,32,126]{3,0,2,1:T(8,128)} %get-tuple-element.28) | copy-start | bytes 2322436
  87.9 24.3 %copy-start.4 = (f32[8,6,32,127]{3,0,2,1:T(8,128)S(1)}, f32[8,6,32,127]{3,0,2,1:T(8,128)}, u32[]{:S(2)}) copy-start(f32[8,6,32,127]{3,0,2,1:T(8,128)} %get-tuple-element.32) | copy-start | bytes 2340868
  87.9 24.3 %copy-start.5 = (f32[8,6,32,127]{3,0,2,1:T(8,128)S(1)}, f32[8,6,32,127]{3,0,2,1:T(8,128)}, u32[]{:S(2)}) copy-start(f32[8,6,32,127]{3,0,2,1:T(8,128)} %get-tuple-element.33) | copy-start | bytes 2340868
  87.9 24.3 %copy-start.6 = (f32[8,6,32,1]{3,0,2,1:T(8,128)S(1)}, f32[8,6,32,1]{3,0,2,1:T(8,128)}, u32[]{:S(2)}) copy-start(f32[8,6,32,1]{3,0,2,1:T(8,128)} %get-tuple-element.34) | copy-start | bytes 18436
  87.9 24.3 %copy-start.7 = (f32[8,6,32,1]{3,0,2,1:T(8,128)S(1)}, f32[8,6,32,1]{3,0,2,1:T(8,128)}, u32[]{:S(2)}) copy-start(f32[8,6,32,1]{3,0,2,1:T(8,128)} %get-tuple-element.35) | copy-start | bytes 18436
  87.9 24.3 %copy-start.9 = (f32[8,6,6,128]{3,0,2,1:T(8,128)S(1)}, f32[8,6,6,128]{3,0,2,1:T(8,128)}, u32[]{:S(2)}) copy-start(f32[8,6,6,128]{3,0,2,1:T(8,128)} %get-tuple-element.39) | copy-start | bytes 442372
  87.9 24.3 %collective-permute-start.2 = (bf16[8,6,32,128]{3,0,2,1:T(8,128)(2,1)S(1)}, bf16[8,6,32,128]{3,0,2,1:T(8,128)(2,1)}, u32[]{:S(2)}, u32[]{:S(2)}) collective-permute-start(bf16[8,6,32,128]{3,0,2,1:T(8,128)(2,1)S(1)} %slice.432), channel_id=1, source_target_pairs={{0,8},{8,16},{16,24},{24,32},{32,40},{40,48},{48,56},{56,64},{64,7... | collective-permute-start | bytes 1179656 | tf_op jit(solution)/shard_map/ppermute | solution.py:41
  124.6 0.7 copy-start.12
  124.6 1.9 copy-start.3
  181.9 225.7 %copy-start.1 = (bf16[4,9,6,32,128]{4,3,2,1,0:T(8,128)(2,1)S(1)}, bf16[4,9,6,32,128]{4,3,2,1,0:T(8,128)(2,1)}, u32[]{:S(2)}) copy-start(bf16[4,9,6,32,128]{4,3,2,1,0:T(8,128)(2,1)} %param.9) | copy-start | bytes 5308420
Sparse Core Ops, SparseCore 0:
  124.8 53.1 all-gather.1
where the time goes:
time: 415 us; the launch traced here: 414 us
  blocking collectives  223 us (54%)
  waiting for transfers between devices  72 us (17%)
  local copies, waits for them, and re-layouts  56.6 us (14%)
  matrix products  17.9 us (4%)
  starting transfers between devices  17.4 us (4%)
  between operations  15 us (4%)
  other arithmetic  12.5 us (3%)
    unnamed x1, blocking collectives  223 us
    all_gather x1, waiting for transfers between devices, shards(): piece = lax.all_gather(filtered, 'band', axis=0, tiled=True)  50.6 us
    slice x24, local copies, waits for them, and re-layouts, laplace_axis(): jnp.roll(field, -offset, axis)  27.1 us
    ppermute x1, waiting for transfers between devices, shifted(): return lax.ppermute(value, axis, pairs)  16.5 us
    convert_element_type x1, other arithmetic, shards(): (2.0 / halfwidth * (hamil - center * orbitals) - previous).astype(jnp.bfl...  12.4 us
    unnamed x38, local copies, waits for them, and re-layouts  9.18 us
  transfers between devices with their start and end apart: 4, of which 4 were waited for; matrix products, arithmetic and copies ran while one was open for 12% of the time, Pallas kernels for 0%

commit v1 on v0

v1 whole, which is shorter than its diff:
```python
import jax
import jax.numpy as jnp
from jax import lax
from jax.experimental import pallas as pl
from jax.experimental.pallas import tpu as pltpu
from jax.sharding import PartitionSpec as P

MESH = pl.DeviceIdType.MESH
BF = jnp.bfloat16
F32 = jnp.float32

HALO = 6
BOX = 6
NPJ = 9
ATOM_DEV = 4
RING = 16
GROUP = 8
COLUMNS = 16
SIDE = 4
SLABS = 32
PAD = BOX - 1
ORDER = (1, 15, 2, 14, 3, 13, 4, 12, 5, 11, 6, 10, 7, 9, 8)

stencil_weights = (
    -5369.0 / 1800.0,
    12.0 / 7.0,
    -15.0 / 56.0,
    10.0 / 189.0,
    -1.0 / 112.0,
    2.0 / 1925.0,
    -1.0 / 16632.0,
)
center = 5.5
halfwidth = 5.5
gain = 2.0 / halfwidth


def nt_dot(a, b):
    return lax.dot_general(a, b, (((1,), (1,)), ((), ())), preferred_element_type=F32)


def step_kernel(
    scale,
    planes_ref,
    psi_ref,
    prev_ref,
    pot_ref,
    own_proj_ref,
    far_proj_ref,
    strength_ref,
    filtered_ref,
    gram_ref,
    psi_send,
    local_send,
    window,
    local_got,
    filt_send,
    proj,
    proj_low,
    along_x,
    coef_acc,
    coef_send,
    coef_got,
    coef_mine,
    coef_all,
    gram_acc,
    gram_y_send,
    gram_y_got,
    gram_x_send,
    gram_x_got,
    gram_z_send,
    gram_z_got,
    psi_ss,
    psi_rs,
    halo_ss,
    halo_rs,
    proj_ss,
    proj_rs,
    local_ss,
    local_rs,
    red_ss,
    red_rs,
    all_ss,
    all_rs,
    filt_ss,
    filt_rs,
    gy_ss,
    gy_rs,
    gx_ss,
    gx_rs,
    gz_ss,
    gz_rs,
):
    space = lax.axis_index("space")
    band = lax.axis_index("band")
    column, half = space // 2, lax.rem(space, 2)
    col_y, col_x = column // SIDE, lax.rem(column, SIDE)
    me = half * GROUP + band

    def ring(k):
        return lax.rem(me + k, RING)

    def at_ring(index):
        return {"space": column * 2 + index // GROUP, "band": lax.rem(index, GROUP)}

    def at_column(col):
        return {"space": lax.rem(col + COLUMNS, COLUMNS) * 2 + half, "band": band}

    def remote(src, dst, ssem, rsem, device):
        return pltpu.make_async_remote_copy(
            src_ref=src, dst_ref=dst, send_sem=ssem, recv_sem=rsem,
            device_id=device, device_id_type=MESH,
        )

    mirror = (1 - half) * GROUP + (3 - band // 2) * 2 + lax.rem(band, 2)

    barrier = pltpu.get_barrier_semaphore()
    peers = [at_ring(ring(k)) for k in ORDER]
    peers += [at_column(lax.rem(col_y + k, SIDE) * SIDE + col_x) for k in (1, 2, 3)]
    peers += [at_column(col_y * SIDE + lax.rem(col_x + k, SIDE)) for k in (1, 2, 3)]
    peers += [at_column(column + 1), at_column(column - 1)]
    for peer in peers:
        pl.semaphore_signal(barrier, inc=1, device_id=peer, device_id_type=MESH)

    def pack(p, carry):
        psi_send[:, p] = psi_ref[p].reshape(RING, 16, 128).astype(BF)
        return carry

    lax.fori_loop(0, HALO, pack, 0)
    for k in range(3):
        table = proj.at[k - 1] if k else proj_low
        table[:, 0:PAD] = jnp.zeros((ATOM_DEV, PAD, 32, 128), BF)
        table[:, PAD + BOX :] = jnp.zeros((ATOM_DEV, BOX, 32, 128), BF)
    proj[half, :, PAD : PAD + BOX] = own_proj_ref[...]
    window[1 + half, band] = psi_send[me]

    pl.semaphore_wait(barrier, len(peers))

    inner = pl.ds(PAD, BOX)
    sends = []
    for k in ORDER:
        copy = remote(
            psi_send.at[ring(k)], window.at[1 + half, band], psi_ss.at[k], psi_rs.at[k],
            at_ring(ring(k)),
        )
        copy.start()
        sends.append(copy)
    copy = remote(
        far_proj_ref, proj.at[half, :, inner], proj_ss.at[0], proj_rs.at[0], at_ring(mirror)
    )
    copy.start()
    sends.append(copy)

    def local_terms(p, carry):
        field = psi_ref[p]
        flat = field.reshape(256, 128)
        total = (3.0 * stencil_weights[0]) * field
        for m in range(1, HALO + 1):
            ahead = jnp.concatenate([field[m:], field[:m]], axis=0)
            behind = jnp.concatenate([field[32 - m :], field[: 32 - m]], axis=0)
            turned = pltpu.roll(flat, m, 1) + pltpu.roll(flat, 128 - m, 1)
            total = total + stencil_weights[m] * (ahead + behind + turned.reshape(32, 8, 128))
        level = pot_ref[p][:, None, :] - center
        local = gain * (level * field - 0.5 * total) - prev_ref[p]
        local_send[:, p] = local.reshape(RING, 16, 128).astype(BF)
        return carry

    lax.fori_loop(0, HALO, local_terms, 0)
    local_got[me] = local_send[me]

    for k in (0,) + ORDER:
        source = lax.rem(me - k + RING, RING)
        side, group = source // GROUP, lax.rem(source, GROUP)
        piece = window.at[1 + side, group]
        if k:
            remote(piece, piece, psi_ss.at[k], psi_rs.at[k], at_ring(source)).wait_recv()
        copy = remote(
            piece, window.at[3 - 3 * side, group], halo_ss.at[k], halo_rs.at[k],
            at_column(column + 2 * side - 1),
        )
        copy.start()
        sends.append(copy)

    remote(
        far_proj_ref, proj.at[1 - half, :, inner], proj_ss.at[0], proj_rs.at[0], at_ring(mirror)
    ).wait_recv()
    copy = remote(
        proj.at[1, :, inner], proj_low.at[:, inner], proj_ss.at[1], proj_rs.at[1],
        at_column(column + 1),
    )
    copy.start()
    sends.append(copy)

    for k in ORDER:
        copy = remote(
            local_send.at[ring(k)], local_got.at[me], local_ss.at[k], local_rs.at[k],
            at_ring(ring(k)),
        )
        copy.start()
        sends.append(copy)

    slabs = [lax.rem(2 * column - 1 + k + SLABS, SLABS) for k in range(3)]

    def start(k, a):
        return jnp.clip(planes_ref[slabs[k] * ATOM_DEV + a] - slabs[k] * HALO, 0, HALO - 1)

    starts = [[start(k, a) for a in range(ATOM_DEV)] for k in range(3)]

    def stack(k, plane):
        table = proj.at[k - 1] if k else proj_low
        rows = [table[a, plane - starts[k][a] + PAD] for a in range(ATOM_DEV)]
        return jnp.concatenate(rows, axis=0)

    def psi_plane(m, p):
        return window[m, :, p].reshape(128, 128)

    coef_acc[...] = jnp.zeros_like(coef_acc)

    def coefs(pairs):
        def body(p, carry):
            for m, k in pairs:
                coef_acc[k] += nt_dot(psi_plane(m, p), stack(k, HALO * (m - k) + p))
            return carry

        lax.fori_loop(0, HALO, body, 0)

    coefs(((1, 1), (2, 1), (2, 2)))
    remote(
        proj.at[1, :, inner], proj_low.at[:, inner], proj_ss.at[1], proj_rs.at[1],
        at_column(column - 1),
    ).wait_recv()
    for k in (0,) + ORDER:
        source = lax.rem(me - k + RING, RING)
        side, group = source // GROUP, lax.rem(source, GROUP)
        slot = window.at[3 - 3 * side, group]
        remote(
            slot, slot, halo_ss.at[k], halo_rs.at[k], at_column(column + 2 * side - 1)
        ).wait_recv()
    coefs(((1, 0), (0, 0), (3, 2)))

    lane = lax.broadcasted_iota(jnp.int32, (GROUP, 8, 128), 2)
    even_row = (lane & 16) == 0

    def swap(value):
        up = pltpu.roll(value, 16, 2)
        down = pltpu.roll(value, 112, 2)
        return jnp.where(even_row, down, up)

    folded = []
    for k in range(3):
        parts = coef_acc[k].reshape(GROUP, 2, 8, 128)
        mixed = jnp.where(even_row, parts[:, 0], parts[:, 1])
        folded.append(mixed + swap(mixed))
    coef_send[0:GROUP] = jnp.where(even_row, folded[0], folded[1])
    coef_send[GROUP:] = folded[2]
    coef_got[me] = coef_send[me]
    for k in ORDER:
        copy = remote(
            coef_send.at[ring(k)], coef_got.at[me], red_ss.at[k], red_rs.at[k], at_ring(ring(k))
        )
        copy.start()
        sends.append(copy)

    def stencil_x(group, carry):
        planes = window[:, group].reshape(24, 16, 128).astype(F32)
        total = jnp.zeros((12, 16, 128), F32)
        for m in range(1, HALO + 1):
            pair = planes[HALO - m : 18 - m] + planes[HALO + m : 18 + m]
            total = total + (-0.5 * gain * stencil_weights[m]) * pair
        along_x[group] = total
        return carry

    lax.fori_loop(0, GROUP, stencil_x, 0)

    for k in ORDER:
        slot = coef_got.at[lax.rem(me - k + RING, RING)]
        remote(slot, slot, red_ss.at[k], red_rs.at[k], at_ring(ring(k))).wait_recv()
    mine = jnp.sum(coef_got[...], axis=0)
    coef_mine[...] = mine
    coef_all[me] = mine
    for k in ORDER:
        copy = remote(coef_mine, coef_all.at[me], all_ss.at[k], all_rs.at[k], at_ring(ring(k)))
        copy.start()
        sends.append(copy)
    gram_acc[...] = jnp.zeros_like(gram_acc)
    for k in ORDER:
        slot = coef_all.at[lax.rem(me - k + RING, RING)]
        remote(coef_mine, slot, all_ss.at[k], all_rs.at[k], at_ring(ring(k))).wait_recv()

    shared = coef_all[0:GROUP]
    crossed = swap(shared)
    full = [
        jnp.where(even_row, shared, crossed),
        jnp.where(even_row, crossed, shared),
        coef_all[GROUP:],
    ]
    weights = []
    for k in range(3):
        weighted = full[k] * (gain * strength_ref[pl.ds(slabs[k], 1)])
        rows = [jnp.where(even_row, weighted, 0.0), jnp.where(even_row, 0.0, weighted)]
        weights.append(jnp.stack(rows, axis=1).reshape(128, 128).astype(BF))

    for k in ORDER:
        slot = local_got.at[lax.rem(me - k + RING, RING)]
        remote(slot, slot, local_ss.at[k], local_rs.at[k], at_ring(ring(k))).wait_recv()

    for m in (1, 2):
        side = m - 1
        both = jnp.concatenate([weights[m - 1], weights[m]], axis=1)
        rows = pl.ds(side * GROUP, GROUP)

        def finish(p, carry):
            table = jnp.concatenate([stack(m - 1, HALO + p), stack(m, p)], axis=0)
            term = jnp.dot(both, table, preferred_element_type=F32)
            term = term + along_x[:, side * HALO + p].reshape(128, 128)
            term = term + local_got[rows, p].reshape(128, 128).astype(F32)
            value = term.astype(BF)
            filt_send[rows, p] = value.reshape(GROUP, 16, 128)
            columns = jnp.concatenate([value, psi_plane(m, p)], axis=0)
            gram_acc[...] += nt_dot(value, columns)
            return carry

        lax.fori_loop(0, HALO, finish, 0)
        for k in ORDER:
            target = ring(k)

            @pl.when(target // GROUP == side)
            def _():
                remote(
                    filt_send.at[target], filtered_ref.at[me], filt_ss.at[k], filt_rs.at[k],
                    at_ring(target),
                ).start()

    filtered_ref[me] = filt_send[me]

    even_eight = (lane & 8) == 0
    parts = gram_acc[...].reshape(GROUP, 2, 8, 256)
    left = jnp.where(even_eight, parts[:, 0, :, :128], parts[:, 1, :, :128])
    right = jnp.where(even_eight, parts[:, 0, :, 128:], parts[:, 1, :, 128:])
    merged = jnp.where(
        even_eight, left + pltpu.roll(left, 120, 2), right + pltpu.roll(right, 8, 2)
    )
    gram_y_send[...] = merged.reshape(SIDE, 16, 128)
    gram_y_got[col_y] = gram_y_send[col_y]
    for k in (1, 3, 2):
        to = lax.rem(col_y + k, SIDE)
        copy = remote(
            gram_y_send.at[to], gram_y_got.at[col_y], gy_ss.at[k], gy_rs.at[k],
            at_column(to * SIDE + col_x),
        )
        copy.start()
        sends.append(copy)
    for k in (1, 3, 2):
        source = lax.rem(col_y - k + SIDE, SIDE)
        slot = gram_y_got.at[source]
        remote(
            slot, slot, gy_ss.at[k], gy_rs.at[k], at_column(source * SIDE + col_x)
        ).wait_recv()
    rows_y = jnp.sum(gram_y_got[...], axis=0)
    for x in range(SIDE):
        block = rows_y[4 * x : 4 * x + 4]
        gram_x_send[x] = jnp.concatenate([block, jnp.zeros((4, 128), F32)], axis=0)
    gram_x_got[col_x] = gram_x_send[col_x]
    for k in (1, 3, 2):
        to = lax.rem(col_x + k, SIDE)
        copy = remote(
            gram_x_send.at[to], gram_x_got.at[col_x], gx_ss.at[k], gx_rs.at[k],
            at_column(col_y * SIDE + to),
        )
        copy.start()
        sends.append(copy)
    for k in (1, 3, 2):
        source = lax.rem(col_x - k + SIDE, SIDE)
        slot = gram_x_got.at[source]
        remote(
            slot, slot, gx_ss.at[k], gx_rs.at[k], at_column(col_y * SIDE + source)
        ).wait_recv()
    rows_x = jnp.sum(gram_x_got[...], axis=0)
    gram_z_send[...] = rows_x
    gram_z_got[me] = rows_x
    for k in ORDER:
        copy = remote(gram_z_send, gram_z_got.at[me], gz_ss.at[k], gz_rs.at[k], at_ring(ring(k)))
        copy.start()
        sends.append(copy)
    for k in ORDER:
        slot = gram_z_got.at[lax.rem(me - k + RING, RING)]
        remote(gram_z_send, slot, gz_ss.at[k], gz_rs.at[k], at_ring(ring(k))).wait_recv()
    gram_ref[...] = jnp.sum(gram_z_got[...], axis=0) * scale

    for k in ORDER:
        copy = remote(
            filt_send.at[ring(k)], filtered_ref.at[lax.rem(me - k + RING, RING)],
            filt_ss.at[k], filt_rs.at[k], at_ring(ring(k)),
        )
        copy.wait_recv()
        copy.wait_send()
    for copy in sends:
        copy.wait_send()


def shards(orbitals, previous, potential, projectors, strengths, atom_planes):
    band_dev, slab_planes, cells_y, cells_z = orbitals.shape
    space_count, band_count = lax.axis_size("space"), lax.axis_size("band")
    cells = slab_planes * space_count * cells_y * cells_z
    half = lax.rem(lax.axis_index("space"), 2)
    band = lax.axis_index("band")
    own = half * GROUP + band
    far = (1 - half) * GROUP + (3 - band // 2) * 2 + lax.rem(band, 2)

    def rows_of(pair):
        piece = lax.dynamic_slice_in_dim(projectors, 2 * pair, 2, 3)
        piece = piece.transpose(0, 2, 3, 1, 4)
        piece = jnp.pad(piece, ((0, 0), (0, 0), (0, 0), (0, 16 - NPJ), (0, 0)))
        return piece.reshape(ATOM_DEV, BOX, 32, cells_z)

    levels = strengths.reshape(SLABS, ATOM_DEV, 1, NPJ)
    levels = jnp.pad(levels, ((0, 0), (0, 0), (0, 0), (0, 16 - NPJ)))
    levels = jnp.broadcast_to(levels, (SLABS, ATOM_DEV, 2, 16)).reshape(SLABS, 128)

    vmem = pl.BlockSpec(memory_space=pltpu.VMEM)
    dma = pltpu.SemaphoreType.DMA
    slab_rows = (RING, HALO, 16, 128)
    tile = (8, 128)
    sems = [RING, RING, RING, RING, 2, 2] + [RING] * 8 + [SIDE] * 4 + [RING] * 2
    filtered, gram = pl.pallas_call(
        lambda *refs: step_kernel(1.0 / cells, *refs),
        out_shape=(
            jax.ShapeDtypeStruct(slab_rows, BF),
            jax.ShapeDtypeStruct(tile, F32),
        ),
        in_specs=[pl.BlockSpec(memory_space=pltpu.SMEM)] + [vmem] * 6,
        out_specs=(vmem, vmem),
        scratch_shapes=[
            pltpu.VMEM(slab_rows, BF),
            pltpu.VMEM(slab_rows, BF),
            pltpu.VMEM((4, GROUP, HALO, 16, 128), BF),
            pltpu.VMEM(slab_rows, BF),
            pltpu.VMEM(slab_rows, BF),
            pltpu.VMEM((2, ATOM_DEV, PAD + 2 * BOX, 32, 128), BF),
            pltpu.VMEM((ATOM_DEV, PAD + 2 * BOX, 32, 128), BF),
            pltpu.VMEM((GROUP, 12, 16, 128), F32),
            pltpu.VMEM((3, 128, 128), F32),
            pltpu.VMEM((RING,) + tile, F32),
            pltpu.VMEM((RING,) + tile, F32),
            pltpu.VMEM(tile, F32),
            pltpu.VMEM((RING,) + tile, F32),
            pltpu.VMEM((128, 256), F32),
            pltpu.VMEM((SIDE, 16, 128), F32),
            pltpu.VMEM((SIDE, 16, 128), F32),
            pltpu.VMEM((SIDE,) + tile, F32),
            pltpu.VMEM((SIDE,) + tile, F32),
            pltpu.VMEM(tile, F32),
            pltpu.VMEM((RING,) + tile, F32),
        ]
        + [dma((n,)) for n in sems],
        compiler_params=pltpu.CompilerParams(
            collective_id=0, has_side_effects=True, vmem_limit_bytes=50 << 20
        ),
        name="filter_step",
    )(
        atom_planes,
        orbitals.transpose(1, 2, 0, 3),
        previous.transpose(1, 2, 0, 3),
        potential,
        rows_of(own),
        rows_of(far),
        levels,
    )
    filtered = filtered.reshape(RING, HALO, 2, band_dev, cells_z)
    filtered = filtered.transpose(3, 1, 0, 2, 4).reshape(orbitals.shape)
    gram = gram[:4].reshape(2, 2, GROUP, 2, 8)
    gram = lax.dynamic_index_in_dim(gram, half, 0, keepdims=False)
    gram = lax.dynamic_index_in_dim(gram, band, 1, keepdims=False)
    return filtered, gram[:, 0], gram[:, 1]


def solution(mesh):
    in_specs = (
        P("band", "space", None, None),
        P("band", "space", None, None),
        P("space", None, None),
        P("space", None, None, None, None),
        P(),
        P(),
    )
    out_specs = (P("band", "space", None, None), P("space", "band"), P("space", "band"))
    return jax.shard_map(
        shards, mesh=mesh, in_specs=in_specs, out_specs=out_specs, check_vma=False
    )
```

time: 415 us -> 75.3 us (0.18)
  the two profiles are of different devices: /device:TPU:32 before, /device:TPU:1 now
where the time goes in v1:
time: 75.3 us; the launch traced here: 75.2 us
  Pallas kernels  68.9 us (92%)
  local copies, waits for them, and re-layouts  5.5 us (7%)
  between operations  0.8 us (1%)
    pallas_call x1, Pallas kernels, shards(): pl.pallas_call(lambda *refs: step_kernel(1.0 / cells, *refs), out_shape=(...  68.9 us

profile of v1, /device:TPU:1, one launch (start us, length us, event | category | flops | bytes accessed | tf_op | source)
XLA Modules:
  0.0 75.2 jit_solution(6472922073318554636)
XLA Ops:
  0.6 0.0 copy-start.2
  0.6 0.0 copy-start.3
  0.7 0.9 %copy.20 = f32[128,9]{1,0:T(8,128)S(1)} copy(f32[128,9]{0,1:T(8,128)} %param.10) | data formatting | bytes 9216 | tf_op args[4]
  1.6 0.1 copy.21
  1.7 0.1 copy.22.refs_6_
  1.8 1.4 %dynamic-slice_bitcast_fusion = (bf16[4,6,2,9,128]{4,2,1,3,0:T(2,128)(2,1)S(1)}, bf16[4,6,2,9,128]{4,2,1,3,0:T(2,128)(2,1)S(1)}) fusion(bf16[4,9,6,32,128]{4,3,2,1,0:T(8,128)(2,1)} %param.9, s32[]{:T(128)S(6)} %select_n.25, s32[]{:T(128)S(6)} %select_n.23), kind=kLoop, calls=%fused_computation.2 | loop fusion | bytes 442376 | tf_op jit(solution)/shard_map/transpose | solution.py:412
  3.3 0.0 copy-start
  3.3 0.0 copy-start.1
  3.4 0.0 copy-done.2
  3.4 0.0 copy-done.3
  3.4 1.1 %copy_bitcast_fusion = (f32[6,32,8,128]{3,2,1,0:T(8,128)S(1)}, f32[6,32,8,128]{3,2,1,0:T(8,128)S(1)}) fusion(f32[8,6,32,128]{3,2,1,0:T(8,128)S(1)} %copy-done.2, f32[8,6,32,128]{3,2,1,0:T(8,128)S(1)} %copy-done.3), kind=kLoop, calls=%fused_computation | loop fusion | bytes 3145728 | tf_op jit(solution)/shard_map/transpose | solution.py:463
  4.5 0.0 copy-done
  4.5 0.0 copy-done.1
  4.5 68.9 %filter_step.1 = (bf16[16,6,16,128]{3,2,1,0:T(8,128)(2,1)S(1)}, f32[8,128]{1,0:T(8,128)S(1)}) custom-call(s32[128]{0:T(128)S(1)} %copy-done.1, f32[6,32,8,128]{3,2,1,0:T(8,128)S(1)} %get-tuple-element.12.refs_1_, f32[6,32,8,128]{3,2,1,0:T(8,128)S(1)} %get-tuple-element.11.refs_2_, f32[6,32,128]{2,1,0:T(8,128)S(1)} %copy-done, ...), custom_call_target="tpu_custom_call" | custom-call | tf_op jit(solution)/shard_map/filter_step/pallas_call | solution.py:425
  73.4 1.1 %copy.23 = bf16[8,6,16,2,128]{4,3,2,1,0:T(2,128)(2,1)} copy(bf16[8,6,16,2,128]{4,0,3,1,2:T(8,128)(2,1)S(1)} %bitcast.26) | data formatting | bytes 786432 | tf_op jit(solution)/shard_map/transpose | solution.py:470
  74.5 0.1 reshape.35
  74.6 0.6 fusion
  (8 shorter events, 0.2 us)
Async XLA Ops:
  0.6 2.8 %copy-start.2 = (f32[8,6,32,128]{3,2,1,0:T(8,128)S(1)}, f32[8,6,32,128]{3,2,1,0:T(8,128)}, u32[]{:S(2)}) copy-start(f32[8,6,32,128]{3,2,1,0:T(8,128)} %param.7) | copy-start | bytes 2359300
  0.6 2.8 %copy-start.3 = (f32[8,6,32,128]{3,2,1,0:T(8,128)S(1)}, f32[8,6,32,128]{3,2,1,0:T(8,128)}, u32[]{:S(2)}) copy-start(f32[8,6,32,128]{3,2,1,0:T(8,128)} %param.6) | copy-start | bytes 2359300
  3.3 1.2 %copy-start = (f32[6,32,128]{2,1,0:T(8,128)S(1)}, f32[6,32,128]{2,1,0:T(8,128)}, u32[]{:S(2)}) copy-start(f32[6,32,128]{2,1,0:T(8,128)} %refs_3_.1) | copy-start | bytes 294916
  3.3 1.2 %copy-start.1 = (s32[128]{0:T(128)S(1)}, s32[128]{0:T(128)}, u32[]{:S(2)}) copy-start(s32[128]{0:T(128)} %refs_0_.1) | copy-start | bytes 1540

commit v2 on v1

--- a/solution.py
+++ b/solution.py
@@ -16,9 +16,10 @@
 RING = 16
 GROUP = 8
 COLUMNS = 16
-SIDE = 4
 SLABS = 32
 PAD = BOX - 1
+ROWS = 2 * BOX * NPJ
+WINDOWS = (0, 96, 208, 304)
 ORDER = (1, 15, 2, 14, 3, 13, 4, 12, 5, 11, 6, 10, 7, 9, 8)
 
 stencil_weights = (
@@ -45,8 +46,8 @@
     psi_ref,
     prev_ref,
     pot_ref,
-    own_proj_ref,
-    far_proj_ref,
+    own_rows_ref,
+    far_rows_ref,
     strength_ref,
     filtered_ref,
     gram_ref,
@@ -57,17 +58,16 @@
     filt_send,
     proj,
     proj_low,
+    far_got,
+    low_got,
+    spread,
     along_x,
-    coef_acc,
     coef_send,
     coef_got,
     coef_mine,
     coef_all,
-    gram_acc,
-    gram_y_send,
-    gram_y_got,
-    gram_x_send,
-    gram_x_got,
+    gram_xy_send,
+    gram_xy_got,
     gram_z_send,
     gram_z_got,
     psi_ss,
@@ -84,17 +84,14 @@
     all_rs,
     filt_ss,
     filt_rs,
-    gy_ss,
-    gy_rs,
-    gx_ss,
-    gx_rs,
+    gxy_ss,
+    gxy_rs,
     gz_ss,
     gz_rs,
 ):
     space = lax.axis_index("space")
     band = lax.axis_index("band")
     column, half = space // 2, lax.rem(space, 2)
-    col_y, col_x = column // SIDE, lax.rem(column, SIDE)
     me = half * GROUP + band
 
     def ring(k):
@@ -116,9 +113,7 @@
 
     barrier = pltpu.get_barrier_semaphore()
     peers = [at_ring(ring(k)) for k in ORDER]
-    peers += [at_column(lax.rem(col_y + k, SIDE) * SIDE + col_x) for k in (1, 2, 3)]
-    peers += [at_column(col_y * SIDE + lax.rem(col_x + k, SIDE)) for k in (1, 2, 3)]
-    peers += [at_column(column + 1), at_column(column - 1)]
+    peers += [at_column(column + k) for k in ORDER]
     for peer in peers:
         pl.semaphore_signal(barrier, inc=1, device_id=peer, device_id_type=MESH)
 
@@ -131,13 +126,36 @@
         table = proj.at[k - 1] if k else proj_low
         table[:, 0:PAD] = jnp.zeros((ATOM_DEV, PAD, 32, 128), BF)
         table[:, PAD + BOX :] = jnp.zeros((ATOM_DEV, BOX, 32, 128), BF)
-    proj[half, :, PAD : PAD + BOX] = own_proj_ref[...]
+
+    row = lax.broadcasted_iota(jnp.int32, (192, 128), 0)
+    source_row = lax.broadcasted_iota(jnp.int32, (192, 128), 1) - 12 * (row & 15) - (row >> 4)
+    for a in range(ATOM_DEV):
+        hit = (source_row == ROWS * a - WINDOWS[a]) & ((row & 15) < NPJ)
+        spread[a] = jnp.where(hit, 1.0, 0.0).astype(BF)
+
+    def expand(rows_ref, table):
+        for a in range(ATOM_DEV):
+            rows = rows_ref[WINDOWS[a] : WINDOWS[a] + 128]
+            moved = jnp.dot(spread[a], rows, preferred_element_type=F32)
+            table[a, PAD : PAD + BOX] = moved.astype(BF).reshape(BOX, 32, 128)
+
+    expand(own_rows_ref, proj.at[half])
     window[1 + half, band] = psi_send[me]
 
     pl.semaphore_wait(barrier, len(peers))
 
-    inner = pl.ds(PAD, BOX)
     sends = []
+    far_copy = remote(far_rows_ref, far_got, proj_ss.at[0], proj_rs.at[0], at_ring(mirror))
+    far_copy.start()
+    sends.append(far_copy)
+
+    def low_copy(rows_ref, col):
+        return remote(rows_ref, low_got, proj_ss.at[1], proj_rs.at[1], at_column(col))
+
+    @pl.when(half == 1)
+    def _():
+        low_copy(own_rows_ref, column + 1).start()
+
     for k in ORDER:
         copy = remote(
             psi_send.at[ring(k)], window.at[1 + half, band], psi_ss.at[k], psi_rs.at[k],
@@ -145,11 +163,6 @@
         )
         copy.start()
         sends.append(copy)
-    copy = remote(
-        far_proj_ref, proj.at[half, :, inner], proj_ss.at[0], proj_rs.at[0], at_ring(mirror)
-    )
-    copy.start()
-    sends.append(copy)
 
     def local_terms(p, carry):
         field = psi_ref[p]
@@ -168,6 +181,12 @@
     lax.fori_loop(0, HALO, local_terms, 0)
     local_got[me] = local_send[me]
 
+    far_copy.wait_recv()
+
+    @pl.when(half == 0)
+    def _():
+        low_copy(far_got, column + 1).start()
+
     for k in (0,) + ORDER:
         source = lax.rem(me - k + RING, RING)
         side, group = source // GROUP, lax.rem(source, GROUP)
@@ -181,16 +200,6 @@
         copy.start()
         sends.append(copy)
 
-    remote(
-        far_proj_ref, proj.at[1 - half, :, inner], proj_ss.at[0], proj_rs.at[0], at_ring(mirror)
-    ).wait_recv()
-    copy = remote(
-        proj.at[1, :, inner], proj_low.at[:, inner], proj_ss.at[1], proj_rs.at[1],
-        at_column(column + 1),
-    )
-    copy.start()
-    sends.append(copy)
-
     for k in ORDER:
         copy = remote(
             local_send.at[ring(k)], local_got.at[me], local_ss.at[k], local_rs.at[k],
@@ -214,21 +223,18 @@
     def psi_plane(m, p):
         return window[m, :, p].reshape(128, 128)
 
-    coef_acc[...] = jnp.zeros_like(coef_acc)
-
-    def coefs(pairs):
-        def body(p, carry):
-            for m, k in pairs:
-                coef_acc[k] += nt_dot(psi_plane(m, p), stack(k, HALO * (m - k) + p))
-            return carry
-
-        lax.fori_loop(0, HALO, body, 0)
-
-    coefs(((1, 1), (2, 1), (2, 2)))
-    remote(
-        proj.at[1, :, inner], proj_low.at[:, inner], proj_ss.at[1], proj_rs.at[1],
-        at_column(column - 1),
-    ).wait_recv()
+    def psi_lanes(m):
+        return jnp.concatenate([psi_plane(m, p) for p in range(HALO)], axis=1)
+
+    def stack_lanes(k, first):
+        return jnp.concatenate([stack(k, first + p) for p in range(HALO)], axis=1)
+
+    expand(far_got, proj.at[1 - half])
+    coef_mid = nt_dot(psi_lanes(1), stack_lanes(1, 0)) + nt_dot(psi_lanes(2), stack_lanes(1, HALO))
+    coef_high = nt_dot(psi_lanes(2), stack_lanes(2, 0))
+    low_copy(far_got, column - 1).wait_recv()
+    expand(low_got, proj_low)
+    coef_low = nt_dot(psi_lanes(1), stack_lanes(0, HALO))
     for k in (0,) + ORDER:
         source = lax.rem(me - k + RING, RING)
         side, group = source // GROUP, lax.rem(source, GROUP)
@@ -236,7 +242,8 @@
         remote(
             slot, slot, halo_ss.at[k], halo_rs.at[k], at_column(column + 2 * side - 1)
         ).wait_recv()
-    coefs(((1, 0), (0, 0), (3, 2)))
+    coef_low = coef_low + nt_dot(psi_lanes(0), stack_lanes(0, 0))
+    coef_high = coef_high + nt_dot(psi_lanes(3), stack_lanes(2, HALO))
 
     lane = lax.broadcasted_iota(jnp.int32, (GROUP, 8, 128), 2)
     even_row = (lane & 16) == 0
@@ -247,8 +254,8 @@
         return jnp.where(even_row, down, up)
 
     folded = []
-    for k in range(3):
-        parts = coef_acc[k].reshape(GROUP, 2, 8, 128)
+    for coef in (coef_low, coef_mid, coef_high):
+        parts = coef.reshape(GROUP, 2, 8, 128)
         mixed = jnp.where(even_row, parts[:, 0], parts[:, 1])
         folded.append(mixed + swap(mixed))
     coef_send[0:GROUP] = jnp.where(even_row, folded[0], folded[1])
@@ -282,7 +289,6 @@
         copy = remote(coef_mine, coef_all.at[me], all_ss.at[k], all_rs.at[k], at_ring(ring(k)))
         copy.start()
         sends.append(copy)
-    gram_acc[...] = jnp.zeros_like(gram_acc)
     for k in ORDER:
         slot = coef_all.at[lax.rem(me - k + RING, RING)]
         remote(coef_mine, slot, all_ss.at[k], all_rs.at[k], at_ring(ring(k))).wait_recv()
@@ -304,23 +310,20 @@
         slot = local_got.at[lax.rem(me - k + RING, RING)]
         remote(slot, slot, local_ss.at[k], local_rs.at[k], at_ring(ring(k))).wait_recv()
 
+    gram = jnp.zeros((128, 256), F32)
     for m in (1, 2):
         side = m - 1
         both = jnp.concatenate([weights[m - 1], weights[m]], axis=1)
         rows = pl.ds(side * GROUP, GROUP)
 
-        def finish(p, carry):
+        values = []
+        for p in range(HALO):
             table = jnp.concatenate([stack(m - 1, HALO + p), stack(m, p)], axis=0)
             term = jnp.dot(both, table, preferred_element_type=F32)
             term = term + along_x[:, side * HALO + p].reshape(128, 128)
             term = term + local_got[rows, p].reshape(128, 128).astype(F32)
-            value = term.astype(BF)
-            filt_send[rows, p] = value.reshape(GROUP, 16, 128)
-            columns = jnp.concatenate([value, psi_plane(m, p)], axis=0)
-            gram_acc[...] += nt_dot(value, columns)
-            return carry
-
-        lax.fori_loop(0, HALO, finish, 0)
+            values.append(term.astype(BF))
+            filt_send[rows, p] = values[p].reshape(GROUP, 16, 128)
         for k in ORDER:
             target = ring(k)
 
@@ -331,51 +334,35 @@
                     at_ring(target),
                 ).start()
 
+        value = jnp.concatenate(values, axis=1)
+        gram = gram + nt_dot(value, jnp.concatenate([value, psi_lanes(m)], axis=0))
+
     filtered_ref[me] = filt_send[me]
 
     even_eight = (lane & 8) == 0
-    parts = gram_acc[...].reshape(GROUP, 2, 8, 256)
+    parts = gram.reshape(GROUP, 2, 8, 256)
     left = jnp.where(even_eight, parts[:, 0, :, :128], parts[:, 1, :, :128])
     right = jnp.where(even_eight, parts[:, 0, :, 128:], parts[:, 1, :, 128:])
     merged = jnp.where(
         even_eight, left + pltpu.roll(left, 120, 2), right + pltpu.roll(right, 8, 2)
     )
-    gram_y_send[...] = merged.reshape(SIDE, 16, 128)
-    gram_y_got[col_y] = gram_y_send[col_y]
-    for k in (1, 3, 2):
-        to = lax.rem(col_y + k, SIDE)
-        copy = remote(
-            gram_y_send.at[to], gram_y_got.at[col_y], gy_ss.at[k], gy_rs.at[k],
-            at_column(to * SIDE + col_x),
-        )
-        copy.start()
-        sends.append(copy)
-    for k in (1, 3, 2):
-        source = lax.rem(col_y - k + SIDE, SIDE)
-        slot = gram_y_got.at[source]
-        remote(
-            slot, slot, gy_ss.at[k], gy_rs.at[k], at_column(source * SIDE + col_x)
-        ).wait_recv()
-    rows_y = jnp.sum(gram_y_got[...], axis=0)
-    for x in range(SIDE):
-        block = rows_y[4 * x : 4 * x + 4]
-        gram_x_send[x] = jnp.concatenate([block, jnp.zeros((4, 128), F32)], axis=0)
-    gram_x_got[col_x] = gram_x_send[col_x]
-    for k in (1, 3, 2):
-        to = lax.rem(col_x + k, SIDE)
-        copy = remote(
-            gram_x_send.at[to], gram_x_got.at[col_x], gx_ss.at[k], gx_rs.at[k],
-            at_column(col_y * SIDE + to),
-        )
-        copy.start()
-        sends.append(copy)
-    for k in (1, 3, 2):
-        source = lax.rem(col_x - k + SIDE, SIDE)
-        slot = gram_x_got.at[source]
-        remote(
-            slot, slot, gx_ss.at[k], gx_rs.at[k], at_column(col_y * SIDE + source)
-        ).wait_recv()
-    rows_x = jnp.sum(gram_x_got[...], axis=0)
+    merged = merged.reshape(64, 128)
+    for c in range(COLUMNS):
+        block = merged[4 * c : 4 * c + 4]
+        gram_xy_send[c] = jnp.concatenate([block, jnp.zeros((4, 128), F32)], axis=0)
+    gram_xy_got[column] = gram_xy_send[column]
+    for k in ORDER:
+        to = lax.rem(column + k, COLUMNS)
+        copy = remote(
+            gram_xy_send.at[to], gram_xy_got.at[column], gxy_ss.at[k], gxy_rs.at[k], at_column(to)
+        )
+        copy.start()
+        sends.append(copy)
+    for k in ORDER:
+        source = lax.rem(column - k + COLUMNS, COLUMNS)
+        slot = gram_xy_got.at[source]
+        remote(slot, slot, gxy_ss.at[k], gxy_rs.at[k], at_column(source)).wait_recv()
+    rows_x = jnp.sum(gram_xy_got[...], axis=0)
     gram_z_send[...] = rows_x
     gram_z_got[me] = rows_x
     for k in ORDER:
@@ -394,6 +381,7 @@
         )
         copy.wait_recv()
         copy.wait_send()
+    low_copy(far_got, column + 1).wait_send()
     for copy in sends:
         copy.wait_send()
 
@@ -409,9 +397,7 @@
 
     def rows_of(pair):
         piece = lax.dynamic_slice_in_dim(projectors, 2 * pair, 2, 3)
-        piece = piece.transpose(0, 2, 3, 1, 4)
-        piece = jnp.pad(piece, ((0, 0), (0, 0), (0, 0), (0, 16 - NPJ), (0, 0)))
-        return piece.reshape(ATOM_DEV, BOX, 32, cells_z)
+        return piece.reshape(ATOM_DEV * ROWS, cells_z)
 
     levels = strengths.reshape(SLABS, ATOM_DEV, 1, NPJ)
     levels = jnp.pad(levels, ((0, 0), (0, 0), (0, 0), (0, 16 - NPJ)))
@@ -421,7 +407,7 @@
     dma = pltpu.SemaphoreType.DMA
     slab_rows = (RING, HALO, 16, 128)
     tile = (8, 128)
-    sems = [RING, RING, RING, RING, 2, 2] + [RING] * 8 + [SIDE] * 4 + [RING] * 2
+    sems = [RING] * 4 + [2, 2] + [RING] * 12
     filtered, gram = pl.pallas_call(
         lambda *refs: step_kernel(1.0 / cells, *refs),
         out_shape=(
@@ -438,17 +424,16 @@
             pltpu.VMEM(slab_rows, BF),
             pltpu.VMEM((2, ATOM_DEV, PAD + 2 * BOX, 32, 128), BF),
             pltpu.VMEM((ATOM_DEV, PAD + 2 * BOX, 32, 128), BF),
+            pltpu.VMEM((ATOM_DEV * ROWS, 128), BF),
+            pltpu.VMEM((ATOM_DEV * ROWS, 128), BF),
+            pltpu.VMEM((ATOM_DEV, 192, 128), BF),
             pltpu.VMEM((GROUP, 12, 16, 128), F32),
-            pltpu.VMEM((3, 128, 128), F32),
             pltpu.VMEM((RING,) + tile, F32),
             pltpu.VMEM((RING,) + tile, F32),
             pltpu.VMEM(tile, F32),
             pltpu.VMEM((RING,) + tile, F32),
-            pltpu.VMEM((128, 256), F32),
-            pltpu.VMEM((SIDE, 16, 128), F32),
-            pltpu.VMEM((SIDE, 16, 128), F32),
-            pltpu.VMEM((SIDE,) + tile, F32),
-            pltpu.VMEM((SIDE,) + tile, F32),
+            pltpu.VMEM((COLUMNS,) + tile, F32),
+            pltpu.VMEM((COLUMNS,) + tile, F32),
             pltpu.VMEM(tile, F32),
             pltpu.VMEM((RING,) + tile, F32),
         ]

time: 75.3 us -> 69.6 us (0.924)
  Pallas kernels: 68.9 us -> 62 us
  local copies, waits for them, and re-layouts: 5.5 us -> 6.63 us
    pallas_call x1, Pallas kernels: 68.9 us -> 62 us  [shards(): pl.pallas_call(lambda *refs: step_kernel(1.0 / cells, *refs), out_shape=(...]
    dynamic_slice x0 -> x1, local copies, waits for them, and re-layouts: none -> 1.45 us  [rows_of(): piece = lax.dynamic_slice_in_dim(projectors, 2 * pair, 2, 3)]
    transpose x1 -> x0, local copies, waits for them, and re-layouts: 1.42 us -> none  [rows_of(): piece = piece.transpose(0, 2, 3, 1, 4)]
    transpose x1, local copies, waits for them, and re-layouts: 1.1 us -> 2.47 us  [shards(): previous.transpose(1, 2, 0, 3)]
where the time goes in v2:
time: 69.6 us; the launch traced here: 69.4 us
  Pallas kernels  62 us (89%)
  local copies, waits for them, and re-layouts  6.63 us (10%)
  between operations  0.72 us (1%)
    pallas_call x1, Pallas kernels, shards(): pl.pallas_call(lambda *refs: step_kernel(1.0 / cells, *refs), out_shape=(...  62 us
    transpose x1, local copies, waits for them, and re-layouts, shards(): previous.transpose(1, 2, 0, 3)  2.47 us
    dynamic_slice x1, local copies, waits for them, and re-layouts, rows_of(): piece = lax.dynamic_slice_in_dim(projectors, 2 * pair, 2, 3)  1.45 us

profile of v2, /device:TPU:1, one launch (start us, length us, event | category | flops | bytes accessed | tf_op | source)
XLA Modules:
  0.0 69.4 jit_solution(18011735057916515970)
XLA Ops:
  0.7 0.8 %copy.16 = f32[128,9]{1,0:T(8,128)S(1)} copy(f32[128,9]{0,1:T(8,128)} %param.10) | data formatting | bytes 9216 | tf_op args[4]
  1.5 0.1 copy.17
  1.6 0.1 copy.18.refs_6_
  1.6 0.0 copy-start
  1.6 0.0 copy-start.1
  1.6 1.5 %constant_dynamic-slice_fusion = (bf16[4,9,6,2,128]{4,3,2,1,0:T(2,128)(2,1)S(1)}, bf16[4,9,6,2,128]{4,3,2,1,0:T(2,128)(2,1)S(1)}) fusion(bf16[4,9,6,32,128]{4,3,2,1,0:T(8,128)(2,1)} %param.9, s32[]{:T(128)S(6)} %select_n.25, s32[]{:T(128)S(6)} %select_n.23), kind=kLoop, calls=%fused_computation.4 | loop fusion | bytes 442376 | tf_op jit(solution)/shard_map/dynamic_slice | solution.py:399
  3.1 2.5 %copy_bitcast_fusion = (f32[6,32,8,128]{3,2,1,0:T(8,128)S(1)}, f32[6,32,8,128]{3,2,1,0:T(8,128)S(1)}) fusion(f32[8,6,32,128]{3,2,1,0:T(8,128)} %param.7, f32[8,6,32,128]{3,2,1,0:T(8,128)} %param.6), kind=kLoop, calls=%fused_computation | loop fusion | bytes 3145728 | tf_op jit(solution)/shard_map/transpose | solution.py:448
  5.6 0.0 copy-done
  5.6 0.0 copy-done.1
  5.6 62.0 %filter_step.1 = (bf16[16,6,16,128]{3,2,1,0:T(8,128)(2,1)S(1)}, f32[8,128]{1,0:T(8,128)S(1)}) custom-call(s32[128]{0:T(128)S(1)} %copy-done.1, f32[6,32,8,128]{3,2,1,0:T(8,128)S(1)} %get-tuple-element.12.refs_1_, f32[6,32,8,128]{3,2,1,0:T(8,128)S(1)} %get-tuple-element.11.refs_2_, f32[6,32,128]{2,1,0:T(8,128)S(1)} %copy-done, bf16[432,128]{1,0:T(8,128)(2,1)S(1)} %bitcast.21, ...), custom_call_target="tpu_custom_call" | custom-call | tf_op jit(solution)/shard_map/filter_step/pallas_call | solution.py:411
  67.6 1.1 %copy.19 = bf16[8,6,16,2,128]{4,3,2,1,0:T(2,128)(2,1)} copy(bf16[8,6,16,2,128]{4,0,3,1,2:T(8,128)(2,1)S(1)} %bitcast.22) | data formatting | bytes 786432 | tf_op jit(solution)/shard_map/transpose | solution.py:455
  68.7 0.1 reshape.35
  68.8 0.6 fusion
  (4 shorter events, 0.0 us)
Async XLA Ops:
  1.6 3.9 %copy-start = (f32[6,32,128]{2,1,0:T(8,128)S(1)}, f32[6,32,128]{2,1,0:T(8,128)}, u32[]{:S(2)}) copy-start(f32[6,32,128]{2,1,0:T(8,128)} %refs_3_.1) | copy-start | bytes 294916
  1.6 3.9 %copy-start.1 = (s32[128]{0:T(128)S(1)}, s32[128]{0:T(128)}, u32[]{:S(2)}) copy-start(s32[128]{0:T(128)} %refs_0_.1) | copy-start | bytes 1540

commit v3 on v2

--- a/solution.py
+++ b/solution.py
@@ -42,15 +42,24 @@
 
 def step_kernel(
     scale,
+    planes_in,
+    psi_in,
+    prev_in,
+    pot_in,
+    proj_ref,
+    strength_in,
+    filtered_ref,
+    gram_ref,
     planes_ref,
     psi_ref,
     prev_ref,
     pot_ref,
-    own_rows_ref,
-    far_rows_ref,
     strength_ref,
-    filtered_ref,
-    gram_ref,
+    psi_rows,
+    near,
+    own_rows,
+    far_rows,
+    pick,
     psi_send,
     local_send,
     window,
@@ -70,6 +79,8 @@
     gram_xy_got,
     gram_z_send,
     gram_z_got,
+    load_sem,
+    near_sem,
     psi_ss,
     psi_rs,
     halo_ss,
@@ -117,8 +128,34 @@
     for peer in peers:
         pl.semaphore_signal(barrier, inc=1, device_id=peer, device_id_type=MESH)
 
+    loads = [
+        pltpu.make_async_copy(source, target, load_sem.at[i])
+        for i, (source, target) in enumerate(
+            (
+                (psi_in, psi_ref),
+                (strength_in, strength_ref),
+                (planes_in, planes_ref),
+                (pot_in, pot_ref),
+                (prev_in, prev_ref),
+            )
+        )
+    ]
+    loads[0].start()
+
+    fetches = []
+    for i, pair in enumerate((me, mirror)):
+        block = pl.ds(pl.multiple_of(pair // 4 * 8, 8), 8)
+        fetch = pltpu.make_async_copy(proj_ref.at[:, :, :, block, :], near.at[i], near_sem.at[i])
+        fetch.start()
+        fetches.append(fetch)
+    for load in loads[1:]:
+        load.start()
+    loads[0].wait()
+
     def pack(p, carry):
-        psi_send[:, p] = psi_ref[p].reshape(RING, 16, 128).astype(BF)
+        turned = jnp.swapaxes(psi_ref[:, p], 0, 1)
+        psi_rows[p] = turned
+        psi_send[:, p] = turned.reshape(RING, 16, 128).astype(BF)
         return carry
 
     lax.fori_loop(0, HALO, pack, 0)
@@ -139,13 +176,41 @@
             moved = jnp.dot(spread[a], rows, preferred_element_type=F32)
             table[a, PAD : PAD + BOX] = moved.astype(BF).reshape(BOX, 32, 128)
 
-    expand(own_rows_ref, proj.at[half])
+    pick_row = lax.broadcasted_iota(jnp.int32, (32, 128), 0)
+    pick_from = lax.broadcasted_iota(jnp.int32, (32, 128), 1)
+    for i, (pair, rows_ref) in enumerate(((mirror, far_rows), (me, own_rows))):
+        wanted = 8 * (pick_row >> 1) + 2 * lax.rem(pair, 4) + (pick_row & 1)
+        pick[i] = jnp.where(pick_from == wanted, 1.0, 0.0).astype(BF)
+        fetches[1 - i].wait()
+        flat = near[1 - i].reshape(ATOM_DEV * ROWS * 4, 128)
+        for g in range(14):
+            first = min(128 * g, ATOM_DEV * ROWS * 4 - 128)
+            rows = jnp.dot(pick[i], flat[first : first + 128], preferred_element_type=F32)
+            rows_ref[first // 4 : first // 4 + 32] = rows.astype(BF)
+
+    expand(own_rows, proj.at[half])
+
+    loads[1].wait()
+    loads[2].wait()
+    lane_row = lax.broadcasted_iota(jnp.int32, (128, 128), 0)
+    lane_col = lax.broadcasted_iota(jnp.int32, (128, 128), 1)
+    own_lane = lax.broadcasted_iota(jnp.int32, (NPJ, 128), 0)
+    own_lane = own_lane == (lax.broadcasted_iota(jnp.int32, (NPJ, 128), 1) & 15)
+    slabs = [lax.rem(2 * column - 1 + k + SLABS, SLABS) for k in range(3)]
+    levels = []
+    for k in range(3):
+        take = jnp.where(lane_row == slabs[k] * ATOM_DEV + (lane_col >> 5), 1.0, 0.0)
+        spread_levels = jnp.dot(
+            strength_ref[...], take, precision=lax.Precision.HIGHEST, preferred_element_type=F32
+        )
+        picked = jnp.where(own_lane, spread_levels, 0.0)
+        levels.append(gain * jnp.sum(picked, axis=0, keepdims=True))
     window[1 + half, band] = psi_send[me]
 
     pl.semaphore_wait(barrier, len(peers))
 
     sends = []
-    far_copy = remote(far_rows_ref, far_got, proj_ss.at[0], proj_rs.at[0], at_ring(mirror))
+    far_copy = remote(far_rows, far_got, proj_ss.at[0], proj_rs.at[0], at_ring(mirror))
     far_copy.start()
     sends.append(far_copy)
 
@@ -154,7 +219,7 @@
 
     @pl.when(half == 1)
     def _():
-        low_copy(own_rows_ref, column + 1).start()
+        low_copy(own_rows, column + 1).start()
 
     for k in ORDER:
         copy = remote(
@@ -164,8 +229,10 @@
         copy.start()
         sends.append(copy)
 
+    loads[3].wait()
+    loads[4].wait()
     def local_terms(p, carry):
-        field = psi_ref[p]
+        field = psi_rows[p]
         flat = field.reshape(256, 128)
         total = (3.0 * stencil_weights[0]) * field
         for m in range(1, HALO + 1):
@@ -174,7 +241,7 @@
             turned = pltpu.roll(flat, m, 1) + pltpu.roll(flat, 128 - m, 1)
             total = total + stencil_weights[m] * (ahead + behind + turned.reshape(32, 8, 128))
         level = pot_ref[p][:, None, :] - center
-        local = gain * (level * field - 0.5 * total) - prev_ref[p]
+        local = gain * (level * field - 0.5 * total) - jnp.swapaxes(prev_ref[:, p], 0, 1)
         local_send[:, p] = local.reshape(RING, 16, 128).astype(BF)
         return carry
 
@@ -207,8 +274,6 @@
         )
         copy.start()
         sends.append(copy)
-
-    slabs = [lax.rem(2 * column - 1 + k + SLABS, SLABS) for k in range(3)]
 
     def start(k, a):
         return jnp.clip(planes_ref[slabs[k] * ATOM_DEV + a] - slabs[k] * HALO, 0, HALO - 1)
@@ -302,7 +367,7 @@
     ]
     weights = []
     for k in range(3):
-        weighted = full[k] * (gain * strength_ref[pl.ds(slabs[k], 1)])
+        weighted = full[k] * levels[k]
         rows = [jnp.where(even_row, weighted, 0.0), jnp.where(even_row, 0.0, weighted)]
         weights.append(jnp.stack(rows, axis=1).reshape(128, 128).astype(BF))
 
@@ -392,31 +457,30 @@
     cells = slab_planes * space_count * cells_y * cells_z
     half = lax.rem(lax.axis_index("space"), 2)
     band = lax.axis_index("band")
-    own = half * GROUP + band
-    far = (1 - half) * GROUP + (3 - band // 2) * 2 + lax.rem(band, 2)
-
-    def rows_of(pair):
-        piece = lax.dynamic_slice_in_dim(projectors, 2 * pair, 2, 3)
-        return piece.reshape(ATOM_DEV * ROWS, cells_z)
-
-    levels = strengths.reshape(SLABS, ATOM_DEV, 1, NPJ)
-    levels = jnp.pad(levels, ((0, 0), (0, 0), (0, 0), (0, 16 - NPJ)))
-    levels = jnp.broadcast_to(levels, (SLABS, ATOM_DEV, 2, 16)).reshape(SLABS, 128)
-
     vmem = pl.BlockSpec(memory_space=pltpu.VMEM)
     dma = pltpu.SemaphoreType.DMA
     slab_rows = (RING, HALO, 16, 128)
     tile = (8, 128)
-    sems = [RING] * 4 + [2, 2] + [RING] * 12
+    sems = [5, 2] + [RING] * 4 + [2, 2] + [RING] * 12
     filtered, gram = pl.pallas_call(
         lambda *refs: step_kernel(1.0 / cells, *refs),
         out_shape=(
             jax.ShapeDtypeStruct(slab_rows, BF),
             jax.ShapeDtypeStruct(tile, F32),
         ),
-        in_specs=[pl.BlockSpec(memory_space=pltpu.SMEM)] + [vmem] * 6,
+        in_specs=[pl.BlockSpec(memory_space=pltpu.HBM)] * 6,
         out_specs=(vmem, vmem),
         scratch_shapes=[
+            pltpu.SMEM(atom_planes.shape, jnp.int32),
+            pltpu.VMEM(orbitals.shape, F32),
+            pltpu.VMEM(orbitals.shape, F32),
+            pltpu.VMEM(potential.shape, F32),
+            pltpu.VMEM(strengths.shape[::-1], F32),
+            pltpu.VMEM((HALO, cells_y, band_dev, cells_z), F32),
+            pltpu.VMEM((2, ATOM_DEV, NPJ, BOX, 8, cells_z), BF),
+            pltpu.VMEM((ATOM_DEV * ROWS, 128), BF),
+            pltpu.VMEM((ATOM_DEV * ROWS, 128), BF),
+            pltpu.VMEM((2, 32, 128), BF),
             pltpu.VMEM(slab_rows, BF),
             pltpu.VMEM(slab_rows, BF),
             pltpu.VMEM((4, GROUP, HALO, 16, 128), BF),
@@ -439,17 +503,16 @@
         ]
         + [dma((n,)) for n in sems],
         compiler_params=pltpu.CompilerParams(
-            collective_id=0, has_side_effects=True, vmem_limit_bytes=50 << 20
+            collective_id=0, has_side_effects=True, vmem_limit_bytes=56 << 20
         ),
         name="filter_step",
     )(
         atom_planes,
-        orbitals.transpose(1, 2, 0, 3),
-        previous.transpose(1, 2, 0, 3),
+        orbitals,
+        previous,
         potential,
-        rows_of(own),
-        rows_of(far),
-        levels,
+        projectors,
+        strengths.T,
     )
     filtered = filtered.reshape(RING, HALO, 2, band_dev, cells_z)
     filtered = filtered.transpose(3, 1, 0, 2, 4).reshape(orbitals.shape)

time: 69.6 us -> 66.6 us (0.957)
  local copies, waits for them, and re-layouts: 6.63 us -> 3.42 us
    transpose x1 -> x0, local copies, waits for them, and re-layouts: 2.47 us -> none  [shards(): previous.transpose(1, 2, 0, 3)]
    dynamic_slice x1 -> x0, local copies, waits for them, and re-layouts: 1.45 us -> none  [rows_of(): piece = lax.dynamic_slice_in_dim(projectors, 2 * pair, 2, 3)]
    transpose x1, local copies, waits for them, and re-layouts: 1.05 us -> 2.04 us  [shards(): filtered = filtered.transpose(3, 1, 0, 2, 4).reshape(orbitals.shape)]
    unnamed x5 -> x0, local copies, waits for them, and re-layouts: 0.81 us -> none
where the time goes in v3:
time: 66.6 us; the launch traced here: 66.4 us
  Pallas kernels  62.3 us (94%)
  local copies, waits for them, and re-layouts  3.42 us (5%)
  between operations  0.67 us (1%)
    pallas_call x1, Pallas kernels, shards(): pl.pallas_call(lambda *refs: step_kernel(1.0 / cells, *refs), out_shape=(...  62.3 us
    transpose x1, local copies, waits for them, and re-layouts, shards(): filtered = filtered.transpose(3, 1, 0, 2, 4).reshape(orbitals.shape)  2.04 us

profile of v3, /device:TPU:1, one launch (start us, length us, event | category | flops | bytes accessed | tf_op | source)
XLA Modules:
  0.0 66.4 jit_solution(15253685566588713105)
XLA Ops:
  0.6 62.3 %filter_step.1 = (bf16[16,6,16,128]{3,2,1,0:T(8,128)(2,1)}, f32[8,128]{1,0:T(8,128)}) custom-call(s32[128]{0:T(128)} %refs_0_.1, f32[8,6,32,128]{3,2,1,0:T(8,128)} %refs_1_.1, f32[8,6,32,128]{3,2,1,0:T(8,128)} %refs_2_.1, f32[6,32,128]{2,1,0:T(8,128)} %refs_3_.1, bf16[4,9,6,32,128]{4,3,2,1,0:T(8,128)(2,1)} %refs_4_.1, f32[9,128]{1,0:T(8,128)} %bitcast.13), custom_call_target="tpu_custom_call" | custom-call | tf_op jit(solution)/shard_map/filter_step/pallas_call | solution.py:465
  63.0 0.7 %slice.9 = f32[4,128]{1,0:T(4,128)S(1)} slice(f32[8,128]{1,0:T(8,128)} %get-tuple-element.6), slice={[0:4], [0:128]} | slice | bytes 4096 | tf_op jit(solution)/shard_map/slice | solution.py:519
  63.7 0.1 reshape.19
  63.8 0.6 fusion
  64.4 2.0 %copy.9 = bf16[8,6,16,2,128]{4,3,2,1,0:T(2,128)(2,1)} copy(bf16[8,6,16,2,128]{4,0,3,1,2:T(8,128)(2,1)} %bitcast.11) | data formatting | bytes 786432 | tf_op jit(solution)/shard_map/transpose | solution.py:518
  (1 shorter events, 0.0 us)

commit v4 on v3

--- a/solution.py
+++ b/solution.py
@@ -20,6 +20,7 @@
 PAD = BOX - 1
 ROWS = 2 * BOX * NPJ
 WINDOWS = (0, 96, 208, 304)
+CHIP_ORDER = (1, 7, 2, 6, 3, 5, 4)
 ORDER = (1, 15, 2, 14, 3, 13, 4, 12, 5, 11, 6, 10, 7, 9, 8)
 
 stencil_weights = (
@@ -59,7 +60,6 @@
     near,
     own_rows,
     far_rows,
-    pick,
     psi_send,
     local_send,
     window,
@@ -72,8 +72,9 @@
     spread,
     along_x,
     coef_send,
+    coef_pair,
+    coef_part,
     coef_got,
-    coef_mine,
     coef_all,
     gram_xy_send,
     gram_xy_got,
@@ -140,16 +141,32 @@
             )
         )
     ]
-    loads[0].start()
-
-    fetches = []
-    for i, pair in enumerate((me, mirror)):
+    fetches = {}
+    for i, pair in ((1, mirror), (0, me)):
         block = pl.ds(pl.multiple_of(pair // 4 * 8, 8), 8)
         fetch = pltpu.make_async_copy(proj_ref.at[:, :, :, block, :], near.at[i], near_sem.at[i])
         fetch.start()
-        fetches.append(fetch)
+        fetches[i] = fetch
+        if i:
+            loads[0].start()
     for load in loads[1:]:
         load.start()
+
+    pick_row = lax.broadcasted_iota(jnp.int32, (32, 128), 0)
+    pick_from = lax.broadcasted_iota(jnp.int32, (32, 128), 1)
+
+    def pick_rows(i, pair, rows_ref):
+        wanted = 8 * (pick_row >> 1) + 2 * lax.rem(pair, 4) + (pick_row & 1)
+        pick = jnp.where(pick_from == wanted, 1.0, 0.0).astype(BF)
+        fetches[i].wait()
+        flat = near[i].reshape(ATOM_DEV * ROWS * 4, 128)
+        for g in range(14):
+            first = min(128 * g, ATOM_DEV * ROWS * 4 - 128)
+            rows = jnp.dot(pick, flat[first : first + 128], preferred_element_type=F32)
+            rows_ref[first // 4 : first // 4 + 32] = rows.astype(BF)
+
+    pick_rows(1, mirror, far_rows)
+
     loads[0].wait()
 
     def pack(p, carry):
@@ -159,6 +176,32 @@
         return carry
 
     lax.fori_loop(0, HALO, pack, 0)
+    window[1 + half, band] = psi_send[me]
+
+    pl.semaphore_wait(barrier, len(peers))
+
+    sends = []
+    far_copy = remote(far_rows, far_got, proj_ss.at[0], proj_rs.at[0], at_ring(mirror))
+
+    def low_copy(rows_ref, col):
+        return remote(rows_ref, low_got, proj_ss.at[1], proj_rs.at[1], at_column(col))
+
+    for k in ORDER:
+        copy = remote(
+            psi_send.at[ring(k)], window.at[1 + half, band], psi_ss.at[k], psi_rs.at[k],
+            at_ring(ring(k)),
+        )
+        copy.start()
+        sends.append(copy)
+
+    far_copy.start()
+    sends.append(far_copy)
+    pick_rows(0, me, own_rows)
+
+    @pl.when(half == 1)
+    def _():
+        low_copy(own_rows, column + 1).start()
+
     for k in range(3):
         table = proj.at[k - 1] if k else proj_low
         table[:, 0:PAD] = jnp.zeros((ATOM_DEV, PAD, 32, 128), BF)
@@ -175,18 +218,6 @@
             rows = rows_ref[WINDOWS[a] : WINDOWS[a] + 128]
             moved = jnp.dot(spread[a], rows, preferred_element_type=F32)
             table[a, PAD : PAD + BOX] = moved.astype(BF).reshape(BOX, 32, 128)
-
-    pick_row = lax.broadcasted_iota(jnp.int32, (32, 128), 0)
-    pick_from = lax.broadcasted_iota(jnp.int32, (32, 128), 1)
-    for i, (pair, rows_ref) in enumerate(((mirror, far_rows), (me, own_rows))):
-        wanted = 8 * (pick_row >> 1) + 2 * lax.rem(pair, 4) + (pick_row & 1)
-        pick[i] = jnp.where(pick_from == wanted, 1.0, 0.0).astype(BF)
-        fetches[1 - i].wait()
-        flat = near[1 - i].reshape(ATOM_DEV * ROWS * 4, 128)
-        for g in range(14):
-            first = min(128 * g, ATOM_DEV * ROWS * 4 - 128)
-            rows = jnp.dot(pick[i], flat[first : first + 128], preferred_element_type=F32)
-            rows_ref[first // 4 : first // 4 + 32] = rows.astype(BF)
 
     expand(own_rows, proj.at[half])
 
@@ -205,29 +236,6 @@
         )
         picked = jnp.where(own_lane, spread_levels, 0.0)
         levels.append(gain * jnp.sum(picked, axis=0, keepdims=True))
-    window[1 + half, band] = psi_send[me]
-
-    pl.semaphore_wait(barrier, len(peers))
-
-    sends = []
-    far_copy = remote(far_rows, far_got, proj_ss.at[0], proj_rs.at[0], at_ring(mirror))
-    far_copy.start()
-    sends.append(far_copy)
-
-    def low_copy(rows_ref, col):
-        return remote(rows_ref, low_got, proj_ss.at[1], proj_rs.at[1], at_column(col))
-
-    @pl.when(half == 1)
-    def _():
-        low_copy(own_rows, column + 1).start()
-
-    for k in ORDER:
-        copy = remote(
-            psi_send.at[ring(k)], window.at[1 + half, band], psi_ss.at[k], psi_rs.at[k],
-            at_ring(ring(k)),
-        )
-        copy.start()
-        sends.append(copy)
 
     loads[3].wait()
     loads[4].wait()
@@ -248,6 +256,14 @@
     lax.fori_loop(0, HALO, local_terms, 0)
     local_got[me] = local_send[me]
 
+    for k in ORDER:
+        copy = remote(
+            local_send.at[ring(k)], local_got.at[me], local_ss.at[k], local_rs.at[k],
+            at_ring(ring(k)),
+        )
+        copy.start()
+        sends.append(copy)
+
     far_copy.wait_recv()
 
     @pl.when(half == 0)
@@ -263,14 +279,6 @@
         copy = remote(
             piece, window.at[3 - 3 * side, group], halo_ss.at[k], halo_rs.at[k],
             at_column(column + 2 * side - 1),
-        )
-        copy.start()
-        sends.append(copy)
-
-    for k in ORDER:
-        copy = remote(
-            local_send.at[ring(k)], local_got.at[me], local_ss.at[k], local_rs.at[k],
-            at_ring(ring(k)),
         )
         copy.start()
         sends.append(copy)
@@ -325,10 +333,20 @@
         folded.append(mixed + swap(mixed))
     coef_send[0:GROUP] = jnp.where(even_row, folded[0], folded[1])
     coef_send[GROUP:] = folded[2]
-    coef_got[me] = coef_send[me]
-    for k in ORDER:
+
+    core = lax.rem(band, 2)
+    chip = me // 2
+    sibling = {"band": band + 1 - 2 * core}
+    kept, given = pl.ds(core * GROUP, GROUP), pl.ds((1 - core) * GROUP, GROUP)
+    copy = remote(coef_send.at[given], coef_pair, red_ss.at[0], red_rs.at[0], sibling)
+    copy.start()
+    sends.append(copy)
+    copy.wait_recv()
+    coef_part[...] = (coef_send[kept] + coef_pair[...]).reshape(4, 16, 128).astype(BF)
+    coef_got[chip] = coef_part[...]
+    for k in CHIP_ORDER:
         copy = remote(
-            coef_send.at[ring(k)], coef_got.at[me], red_ss.at[k], red_rs.at[k], at_ring(ring(k))
+            coef_part, coef_got.at[chip], all_ss.at[k], all_rs.at[k], at_ring(ring(2 * k))
         )
         copy.start()
         sends.append(copy)
@@ -344,19 +362,14 @@
 
     lax.fori_loop(0, GROUP, stencil_x, 0)
 
-    for k in ORDER:
-        slot = coef_got.at[lax.rem(me - k + RING, RING)]
-        remote(slot, slot, red_ss.at[k], red_rs.at[k], at_ring(ring(k))).wait_recv()
-    mine = jnp.sum(coef_got[...], axis=0)
-    coef_mine[...] = mine
-    coef_all[me] = mine
-    for k in ORDER:
-        copy = remote(coef_mine, coef_all.at[me], all_ss.at[k], all_rs.at[k], at_ring(ring(k)))
-        copy.start()
-        sends.append(copy)
-    for k in ORDER:
-        slot = coef_all.at[lax.rem(me - k + RING, RING)]
-        remote(coef_mine, slot, all_ss.at[k], all_rs.at[k], at_ring(ring(k))).wait_recv()
+    for k in CHIP_ORDER:
+        slot = coef_got.at[lax.rem(chip - k + 8, 8)]
+        remote(slot, slot, all_ss.at[k], all_rs.at[k], at_ring(ring(2 * k))).wait_recv()
+    coef_all[kept] = jnp.sum(coef_got[...].astype(F32), axis=0).reshape(GROUP, 8, 128)
+    copy = remote(coef_all.at[kept], coef_all.at[kept], red_ss.at[1], red_rs.at[1], sibling)
+    copy.start()
+    sends.append(copy)
+    remote(coef_all.at[given], coef_all.at[given], red_ss.at[1], red_rs.at[1], sibling).wait_recv()
 
     shared = coef_all[0:GROUP]
     crossed = swap(shared)
@@ -480,7 +493,6 @@
             pltpu.VMEM((2, ATOM_DEV, NPJ, BOX, 8, cells_z), BF),
             pltpu.VMEM((ATOM_DEV * ROWS, 128), BF),
             pltpu.VMEM((ATOM_DEV * ROWS, 128), BF),
-            pltpu.VMEM((2, 32, 128), BF),
             pltpu.VMEM(slab_rows, BF),
             pltpu.VMEM(slab_rows, BF),
             pltpu.VMEM((4, GROUP, HALO, 16, 128), BF),
@@ -493,8 +505,9 @@
             pltpu.VMEM((ATOM_DEV, 192, 128), BF),
             pltpu.VMEM((GROUP, 12, 16, 128), F32),
             pltpu.VMEM((RING,) + tile, F32),
-            pltpu.VMEM((RING,) + tile, F32),
-            pltpu.VMEM(tile, F32),
+            pltpu.VMEM((GROUP,) + tile, F32),
+            pltpu.VMEM((4, 16, 128), BF),
+            pltpu.VMEM((8, 4, 16, 128), BF),
             pltpu.VMEM((RING,) + tile, F32),
             pltpu.VMEM((COLUMNS,) + tile, F32),
             pltpu.VMEM((COLUMNS,) + tile, F32),
@@ -503,16 +516,16 @@
         ]
         + [dma((n,)) for n in sems],
         compiler_params=pltpu.CompilerParams(
-            collective_id=0, has_side_effects=True, vmem_limit_bytes=56 << 20
+            collective_id=0, has_side_effects=True, vmem_limit_bytes=50 << 20
         ),
         name="filter_step",
     )(
-        atom_planes,
-        orbitals,
-        previous,
-        potential,
-        projectors,
-        strengths.T,
+        *(
+            pltpu.with_memory_space_constraint(operand, pltpu.HBM)
+            for operand in (
+                atom_planes, orbitals, previous, potential, projectors, strengths.T
+            )
+        )
     )
     filtered = filtered.reshape(RING, HALO, 2, band_dev, cells_z)
     filtered = filtered.transpose(3, 1, 0, 2, 4).reshape(orbitals.shape)

time: 66.6 us -> 62.6 us (0.940)
  Pallas kernels: 62.3 us -> 60 us
  local copies, waits for them, and re-layouts: 3.42 us -> 1.74 us
    pallas_call x1, Pallas kernels: 62.3 us -> 60 us  [shards(): pl.pallas_call(lambda *refs: step_kernel(1.0 / cells, *refs), out_shape=(...]
    transpose x1, local copies, waits for them, and re-layouts: 2.04 us -> 1.05 us  [shards(): filtered = filtered.transpose(3, 1, 0, 2, 4).reshape(orbitals.shape)]
    slice x1, local copies, waits for them, and re-layouts: 0.68 us -> 0.01 us  [shards(): gram = gram[:4].reshape(2, 2, GROUP, 2, 8)]
where the time goes in v4:
time: 62.6 us; the launch traced here: 62.5 us
  Pallas kernels  60 us (96%)
  local copies, waits for them, and re-layouts  1.74 us (3%)
  between operations  0.68 us (1%)
    pallas_call x1, Pallas kernels, shards(): pl.pallas_call(lambda *refs: step_kernel(1.0 / cells, *refs), out_shape=(...  60 us

profile of v4, /device:TPU:1, one launch (start us, length us, event | category | flops | bytes accessed | tf_op | source)
XLA Modules:
  0.0 62.5 jit_solution(13896902977454438134)
XLA Ops:
  0.6 60.0 %filter_step.1 = (bf16[16,6,16,128]{3,2,1,0:T(8,128)(2,1)S(1)}, f32[8,128]{1,0:T(8,128)S(1)}) custom-call(s32[128]{0:T(128)} %refs_0_.1, f32[8,6,32,128]{3,2,1,0:T(8,128)} %refs_1_.1, f32[8,6,32,128]{3,2,1,0:T(8,128)} %refs_2_.1, f32[6,32,128]{2,1,0:T(8,128)} %refs_3_.1, bf16[4,9,6,32,128]{4,3,2,1,0:T(8,128)(2,1)} %refs_4_.1, f32[9,128]{1,0:T(8,128)} %bitcast.13), custom_call_target="tpu_custom_call" | custom-call | tf_op jit(solution)/shard_map/filter_step/pallas_call | solution.py:478
  60.7 0.1 reshape.19
  60.8 0.6 fusion
  61.4 1.0 %copy.9 = bf16[8,6,16,2,128]{4,3,2,1,0:T(2,128)(2,1)} copy(bf16[8,6,16,2,128]{4,0,3,1,2:T(8,128)(2,1)S(1)} %bitcast.11) | data formatting | bytes 786432 | tf_op jit(solution)/shard_map/transpose | solution.py:531
  (2 shorter events, 0.0 us)

commit v5 on v4

--- a/solution.py
+++ b/solution.py
@@ -20,8 +20,8 @@
 PAD = BOX - 1
 ROWS = 2 * BOX * NPJ
 WINDOWS = (0, 96, 208, 304)
-CHIP_ORDER = (1, 7, 2, 6, 3, 5, 4)
-ORDER = (1, 15, 2, 14, 3, 13, 4, 12, 5, 11, 6, 10, 7, 9, 8)
+CHIP_ORDER = (4, 3, 5, 2, 6, 1, 7)
+ORDER = (8, 9, 7, 6, 10, 5, 11, 4, 12, 3, 13, 2, 14, 1, 15)
 
 stencil_weights = (
     -5369.0 / 1800.0,
@@ -186,6 +186,14 @@
     def low_copy(rows_ref, col):
         return remote(rows_ref, low_got, proj_ss.at[1], proj_rs.at[1], at_column(col))
 
+    far_copy.start()
+    sends.append(far_copy)
+    pick_rows(0, me, own_rows)
+
+    @pl.when(half == 1)
+    def _():
+        low_copy(own_rows, column + 1).start()
+
     for k in ORDER:
         copy = remote(
             psi_send.at[ring(k)], window.at[1 + half, band], psi_ss.at[k], psi_rs.at[k],
@@ -193,14 +201,6 @@
         )
         copy.start()
         sends.append(copy)
-
-    far_copy.start()
-    sends.append(far_copy)
-    pick_rows(0, me, own_rows)
-
-    @pl.when(half == 1)
-    def _():
-        low_copy(own_rows, column + 1).start()
 
     for k in range(3):
         table = proj.at[k - 1] if k else proj_low
@@ -450,7 +450,9 @@
     for k in ORDER:
         slot = gram_z_got.at[lax.rem(me - k + RING, RING)]
         remote(gram_z_send, slot, gz_ss.at[k], gz_rs.at[k], at_ring(ring(k))).wait_recv()
-    gram_ref[...] = jnp.sum(gram_z_got[...], axis=0) * scale
+    total = jnp.sum(gram_z_got[...], axis=0) * scale
+    total = pltpu.roll(total, lax.rem(128 - 16 * band, 128), 1)
+    gram_ref[...] = jnp.where(half == 0, total, pltpu.roll(total, 6, 0))
 
     for k in ORDER:
         copy = remote(
@@ -468,8 +470,6 @@
     band_dev, slab_planes, cells_y, cells_z = orbitals.shape
     space_count, band_count = lax.axis_size("space"), lax.axis_size("band")
     cells = slab_planes * space_count * cells_y * cells_z
-    half = lax.rem(lax.axis_index("space"), 2)
-    band = lax.axis_index("band")
     vmem = pl.BlockSpec(memory_space=pltpu.VMEM)
     dma = pltpu.SemaphoreType.DMA
     slab_rows = (RING, HALO, 16, 128)
@@ -529,10 +529,7 @@
     )
     filtered = filtered.reshape(RING, HALO, 2, band_dev, cells_z)
     filtered = filtered.transpose(3, 1, 0, 2, 4).reshape(orbitals.shape)
-    gram = gram[:4].reshape(2, 2, GROUP, 2, 8)
-    gram = lax.dynamic_index_in_dim(gram, half, 0, keepdims=False)
-    gram = lax.dynamic_index_in_dim(gram, band, 1, keepdims=False)
-    return filtered, gram[:, 0], gram[:, 1]
+    return filtered, gram[:2, :8], gram[:2, 8:16]
 
 
 def solution(mesh):

time: 62.6 us -> 60.8 us (0.971)
  Pallas kernels: 60 us -> 58.4 us
    pallas_call x1, Pallas kernels: 60 us -> 58.4 us  [shards(): pl.pallas_call(lambda *refs: step_kernel(1.0 / cells, *refs), out_shape=(...]
where the time goes in v5:
time: 60.8 us; the launch traced here: 60.7 us
  Pallas kernels  58.4 us (96%)
  local copies, waits for them, and re-layouts  1.68 us (3%)
  between operations  0.64 us (1%)
    pallas_call x1, Pallas kernels, shards(): pl.pallas_call(lambda *refs: step_kernel(1.0 / cells, *refs), out_shape=(...  58.4 us

profile of v5, /device:TPU:1, one launch (start us, length us, event | category | flops | bytes accessed | tf_op | source)
XLA Modules:
  0.0 60.7 jit_solution(5618245499572639359)
XLA Ops:
  0.6 58.4 %filter_step.1 = (bf16[16,6,16,128]{3,2,1,0:T(8,128)(2,1)S(1)}, f32[8,128]{1,0:T(8,128)S(1)}) custom-call(s32[128]{0:T(128)} %refs_0_.1, f32[8,6,32,128]{3,2,1,0:T(8,128)} %refs_1_.1, f32[8,6,32,128]{3,2,1,0:T(8,128)} %refs_2_.1, f32[6,32,128]{2,1,0:T(8,128)} %refs_3_.1, bf16[4,9,6,32,128]{4,3,2,1,0:T(8,128)(2,1)} %refs_4_.1, f32[9,128]{1,0:T(8,128)} %bitcast.7), custom_call_target="tpu_custom_call" | custom-call | tf_op jit(solution)/shard_map/filter_step/pallas_call | solution.py:478
  59.1 0.6 %fusion = (f32[2,8]{1,0:T(2,128)}, f32[2,8]{1,0:T(2,128)}) fusion(f32[8,128]{1,0:T(8,128)S(1)} %get-tuple-element.6), kind=kLoop, calls=%fused_computation | loop fusion | bytes 256 | tf_op jit(solution)/shard_map/slice | solution.py:532
  59.7 1.0 %copy.9 = bf16[8,6,16,2,128]{4,3,2,1,0:T(2,128)(2,1)} copy(bf16[8,6,16,2,128]{4,0,3,1,2:T(8,128)(2,1)S(1)} %bitcast.5) | data formatting | bytes 786432 | tf_op jit(solution)/shard_map/transpose | solution.py:531

commit v6 on v5

--- a/solution.py
+++ b/solution.py
@@ -256,7 +256,7 @@
     lax.fori_loop(0, HALO, local_terms, 0)
     local_got[me] = local_send[me]
 
-    for k in ORDER:
+    for k in (1, 15, 2, 14, 3, 13, 4, 12, 5, 11, 6, 10, 7, 9, 8):
         copy = remote(
             local_send.at[ring(k)], local_got.at[me], local_ss.at[k], local_rs.at[k],
             at_ring(ring(k)),
@@ -426,8 +426,7 @@
     )
     merged = merged.reshape(64, 128)
     for c in range(COLUMNS):
-        block = merged[4 * c : 4 * c + 4]
-        gram_xy_send[c] = jnp.concatenate([block, jnp.zeros((4, 128), F32)], axis=0)
+        gram_xy_send[c] = merged[4 * c : 4 * c + 4]
     gram_xy_got[column] = gram_xy_send[column]
     for k in ORDER:
         to = lax.rem(column + k, COLUMNS)
@@ -451,6 +450,7 @@
         slot = gram_z_got.at[lax.rem(me - k + RING, RING)]
         remote(gram_z_send, slot, gz_ss.at[k], gz_rs.at[k], at_ring(ring(k))).wait_recv()
     total = jnp.sum(gram_z_got[...], axis=0) * scale
+    total = jnp.concatenate([total, total], axis=0)
     total = pltpu.roll(total, lax.rem(128 - 16 * band, 128), 1)
     gram_ref[...] = jnp.where(half == 0, total, pltpu.roll(total, 6, 0))
 
@@ -509,10 +509,10 @@
             pltpu.VMEM((4, 16, 128), BF),
             pltpu.VMEM((8, 4, 16, 128), BF),
             pltpu.VMEM((RING,) + tile, F32),
-            pltpu.VMEM((COLUMNS,) + tile, F32),
-            pltpu.VMEM((COLUMNS,) + tile, F32),
-            pltpu.VMEM(tile, F32),
-            pltpu.VMEM((RING,) + tile, F32),
+            pltpu.VMEM((COLUMNS, 4, 128), F32),
+            pltpu.VMEM((COLUMNS, 4, 128), F32),
+            pltpu.VMEM((4, 128), F32),
+            pltpu.VMEM((RING, 4, 128), F32),
         ]
         + [dma((n,)) for n in sems],
         compiler_params=pltpu.CompilerParams(

time: 60.8 us -> 58.8 us (0.967)
  Pallas kernels: 58.4 us -> 56.4 us
    pallas_call x1, Pallas kernels: 58.4 us -> 56.4 us  [shards(): pl.pallas_call(lambda *refs: step_kernel(1.0 / cells, *refs), out_shape=(...]
where the time goes in v6:
time: 58.8 us; the launch traced here: 58.7 us
  Pallas kernels  56.4 us (96%)
  local copies, waits for them, and re-layouts  1.68 us (3%)
  between operations  0.64 us (1%)
    pallas_call x1, Pallas kernels, shards(): pl.pallas_call(lambda *refs: step_kernel(1.0 / cells, *refs), out_shape=(...  56.4 us

profile of v6, /device:TPU:1, one launch (start us, length us, event | category | flops | bytes accessed | tf_op | source)
XLA Modules:
  0.0 58.7 jit_solution(1906391894382624881)
XLA Ops:
  0.6 56.4 %filter_step.1 = (bf16[16,6,16,128]{3,2,1,0:T(8,128)(2,1)S(1)}, f32[8,128]{1,0:T(8,128)S(1)}) custom-call(s32[128]{0:T(128)} %refs_0_.1, f32[8,6,32,128]{3,2,1,0:T(8,128)} %refs_1_.1, f32[8,6,32,128]{3,2,1,0:T(8,128)} %refs_2_.1, f32[6,32,128]{2,1,0:T(8,128)} %refs_3_.1, bf16[4,9,6,32,128]{4,3,2,1,0:T(8,128)(2,1)} %refs_4_.1, f32[9,128]{1,0:T(8,128)} %bitcast.7), custom_call_target="tpu_custom_call" | custom-call | tf_op jit(solution)/shard_map/filter_step/pallas_call | solution.py:478
  57.0 0.6 %fusion = (f32[2,8]{1,0:T(2,128)}, f32[2,8]{1,0:T(2,128)}) fusion(f32[8,128]{1,0:T(8,128)S(1)} %get-tuple-element.6), kind=kLoop, calls=%fused_computation | loop fusion | bytes 256 | tf_op jit(solution)/shard_map/slice | solution.py:532
  57.7 1.0 %copy.9 = bf16[8,6,16,2,128]{4,3,2,1,0:T(2,128)(2,1)} copy(bf16[8,6,16,2,128]{4,0,3,1,2:T(8,128)(2,1)S(1)} %bitcast.5) | data formatting | bytes 786432 | tf_op jit(solution)/shard_map/transpose | solution.py:531

commit v7 on v6

--- a/solution.py
+++ b/solution.py
@@ -256,7 +256,7 @@
     lax.fori_loop(0, HALO, local_terms, 0)
     local_got[me] = local_send[me]
 
-    for k in (1, 15, 2, 14, 3, 13, 4, 12, 5, 11, 6, 10, 7, 9, 8):
+    for k in (1, 15, 2, 14, 3, 13, 4, 12, 5, 11):
         copy = remote(
             local_send.at[ring(k)], local_got.at[me], local_ss.at[k], local_rs.at[k],
             at_ring(ring(k)),
@@ -279,6 +279,14 @@
         copy = remote(
             piece, window.at[3 - 3 * side, group], halo_ss.at[k], halo_rs.at[k],
             at_column(column + 2 * side - 1),
+        )
+        copy.start()
+        sends.append(copy)
+
+    for k in (6, 10, 7, 9, 8):
+        copy = remote(
+            local_send.at[ring(k)], local_got.at[me], local_ss.at[k], local_rs.at[k],
+            at_ring(ring(k)),
         )
         copy.start()
         sends.append(copy)

time: 58.8 us -> 58.1 us (0.988)
  Pallas kernels: 56.4 us -> 55.6 us
    pallas_call x1, Pallas kernels: 56.4 us -> 55.6 us  [shards(): pl.pallas_call(lambda *refs: step_kernel(1.0 / cells, *refs), out_shape=(...]
where the time goes in v7:
time: 58.1 us; the launch traced here: 58 us
  Pallas kernels  55.6 us (96%)
  local copies, waits for them, and re-layouts  1.68 us (3%)
  between operations  0.64 us (1%)
    pallas_call x1, Pallas kernels, shards(): pl.pallas_call(lambda *refs: step_kernel(1.0 / cells, *refs), out_shape=(...  55.6 us

profile of v7, /device:TPU:1, one launch (start us, length us, event | category | flops | bytes accessed | tf_op | source)
XLA Modules:
  0.0 58.0 jit_solution(8389208036082581426)
XLA Ops:
  0.6 55.6 %filter_step.1 = (bf16[16,6,16,128]{3,2,1,0:T(8,128)(2,1)S(1)}, f32[8,128]{1,0:T(8,128)S(1)}) custom-call(s32[128]{0:T(128)} %refs_0_.1, f32[8,6,32,128]{3,2,1,0:T(8,128)} %refs_1_.1, f32[8,6,32,128]{3,2,1,0:T(8,128)} %refs_2_.1, f32[6,32,128]{2,1,0:T(8,128)} %refs_3_.1, bf16[4,9,6,32,128]{4,3,2,1,0:T(8,128)(2,1)} %refs_4_.1, f32[9,128]{1,0:T(8,128)} %bitcast.7), custom_call_target="tpu_custom_call" | custom-call | tf_op jit(solution)/shard_map/filter_step/pallas_call | solution.py:486
  56.3 0.6 %fusion = (f32[2,8]{1,0:T(2,128)}, f32[2,8]{1,0:T(2,128)}) fusion(f32[8,128]{1,0:T(8,128)S(1)} %get-tuple-element.6), kind=kLoop, calls=%fused_computation | loop fusion | bytes 256 | tf_op jit(solution)/shard_map/slice | solution.py:540
  56.9 1.0 %copy.9 = bf16[8,6,16,2,128]{4,3,2,1,0:T(2,128)(2,1)} copy(bf16[8,6,16,2,128]{4,0,3,1,2:T(8,128)(2,1)S(1)} %bitcast.5) | data formatting | bytes 786432 | tf_op jit(solution)/shard_map/transpose | solution.py:539
